TPU v7x, 32 devices: a whole 2x2x4 slice. The times are simulated.
32 devices in a mesh: weld: 8 (over y, x, core), trans: 4 (over z).
Axes of the slice: x: 2, y: 2, z: 4, core: 2. Of those that a mesh axis runs over, the one named last changes fastest.
Arguments:
- features: bfloat16 [64, 128, 16, 128], P('weld', 'trans'), as said below
- pair_offsets: int32 [64, 128, 12], P('weld', 'trans'), may hold values from 0 to 8
- pair_kernel: int32 [64, 128, 12], P('weld', 'trans'), may hold values from 0 to 15
- kernels: bfloat16 [16, 128, 128], replicated
- send_list: int32 [8, 4, 4, 32], P('weld', 'trans'), may hold values from 0 to 256, as said below
- wall_slots: int32 [8, 4, 16, 16], P('weld', 'trans'), may hold values from 0 to 128, as said below
- wall_kernel: int32 [8, 4, 16, 16], P('weld', 'trans'), may hold values from 0 to 7
- wall_kernels: bfloat16 [8, 128, 128], replicated, as said below
Outputs:
- rates: bfloat16 [64, 128, 16, 128], P('weld', 'trans')
- walls: bfloat16 [8, 4, 16, 16, 128], P('weld', 'trans')
Inputs may be any that keep to these rules, and one draw needn't show every extreme that they name: `send_list`: A value of 256 marks an empty slot; on each device one wall owner gets all 32 slots and every other owner gets fewer. `wall_slots`: A value of 128 reads the zero tile. `features`: channel 0 is positive. `wall_kernels`: entries are non-negative.
All inputs are finite; a program needn't handle non-finite values.
Results may differ from a plain program's by a relative error of at most 0.0075.
Values may be sent and summed in bfloat16 or wider, within the bound.
No kernel may reach another device: no remote copies, remote signals or barrier semaphores. Data moves between devices by JAX's collectives and lax.ppermute only.
A program may use at most 64 MiB of HBM per device.

v0:
```python
import functools

import jax
import jax.numpy as jnp
from jax import lax
from jax.experimental import pallas as pl
from jax.experimental.pallas import tpu as pltpu
from jax.sharding import PartitionSpec as P

SMEM = pl.BlockSpec(memory_space=pltpu.SMEM)
VMEM = pl.BlockSpec(memory_space=pltpu.VMEM)
HBM = pl.BlockSpec(memory_space=pl.ANY)
MIB = 1 << 20
UNROLLED = False


def pick(cond, a, b):
    return lax.select(cond, jnp.int32(a), jnp.int32(b))


def index_kernel(dims, off_ref, kind_ref, slot_ref, wkind_ref, local_ref, side_ref, wall_ref):
    gw, gt, bank, wall_bank, peers, cap = dims
    t = lax.axis_index("trans")
    off, kind = off_ref[...], kind_ref[...]
    dr = (off * 11) >> 5
    row = lax.broadcasted_iota(jnp.int32, off.shape, 1)
    band = row + dr - jnp.where(row < gw // 2, 0, gw // 2)
    col = lax.broadcasted_iota(jnp.int32, off.shape, 2) + (off - 3 * dr) - 1
    left, right = col < 0, col >= gt
    side = left | right
    rows = gw // 2 + 2
    local_ref[:, :, :gt] = jnp.where(
        side, bank * rows * gt, kind * (rows * gt) + band * gt + col
    )
    even_t = lax.rem(t, 2) == 0
    depth = gw + 2
    base = jnp.where(left, pick(even_t, depth, 0), pick(even_t, 0, depth))
    edge = (left & (t == 0)) | (right & (t == peers - 1))
    side_ref[:, :, :gt] = jnp.where(
        side & ~edge, kind * (2 * depth) + base + row + dr, bank * 2 * depth
    )
    slot = slot_ref[...]
    sender = slot // cap
    wall_ref[...] = jnp.where(
        slot >= peers * cap,
        wall_bank * peers * cap,
        wkind_ref[...] * (peers * cap) + (sender ^ t) * cap + (slot - sender * cap),
    )


def load_tiles(x_ref, held_ref, sem):
    count = x_ref.shape[0]
    return pltpu.make_async_copy(x_ref, held_ref.at[:count], sem)


def blank(ref):
    ref[ref.shape[0] - 1] = jnp.zeros(ref.shape[1:], ref.dtype)


def listed(held_ref, list_ref, owner, out_ref):
    for c in range(list_ref.shape[1]):
        out_ref[c] = held_ref[list_ref[owner, c]]


def first_kernel(dims, early, list_ref, x_ref, near_ref, far_ref, *refs):
    gw, gt = dims
    outs, (held_ref, sem) = refs[: len(early)], refs[len(early) :]
    w, t = lax.axis_index("weld"), lax.axis_index("trans")
    even = lax.rem(w, 2) == 0
    load = load_tiles(x_ref, held_ref, sem.at[0])
    load.start()
    rows = []
    for i, (ref, row) in enumerate(
        ((near_ref, pick(even, gw - 1, 0)), (far_ref, pick(even, 0, gw - 1)))
    ):
        rows.append(
            pltpu.make_async_copy(x_ref.at[pl.ds(row * gt, gt)], ref, sem.at[1 + i])
        )
        rows[i].start()
    blank(held_ref)
    load.wait()
    for k, ref in zip(early, outs):
        listed(held_ref, list_ref, t ^ k, ref)
    for copy in rows:
        copy.wait()


def second_kernel(dims, late, merged, list_ref, x_ref, near_ref, far_ref, *refs):
    gw, gt, cap = dims
    outs, (held_ref, sem, corner_sem) = refs[:-3], refs[-3:]
    w, t = lax.axis_index("weld"), lax.axis_index("trans")
    load = load_tiles(x_ref, held_ref, sem)
    load.start()
    blank(held_ref)
    corners, columns = [], []
    even_w, even_t = lax.rem(w, 2) == 0, lax.rem(t, 2) == 0
    for which in range(2):
        if merged:
            ref, base = outs[late.index((1, 3)[which])], cap
        else:
            ref, base = outs[len(late) + which], 0
        column = pick(even_t, gt - 1, 0) if which == 0 else pick(even_t, 0, gt - 1)
        for i, (corner, place) in enumerate(
            ((near_ref, pick(even_w, gw + 1, 0)), (far_ref, pick(even_w, 0, gw + 1)))
        ):
            copy = pltpu.make_async_copy(
                corner.at[column], ref.at[base + place], corner_sem.at[2 * which + i]
            )
            copy.start()
            corners.append(copy)
        columns.append((ref, base, column))
    load.wait()
    for ref, base, column in columns:
        for r in range(gw):
            ref[base + 1 + r] = held_ref[r * gt + column]
    for k, ref in zip(late, outs):
        listed(held_ref, list_ref, t ^ k, ref)
    for copy in corners:
        copy.wait()


def tree(terms):
    while len(terms) > 1:
        terms = [sum(terms[i : i + 2][1:], terms[i]) for i in range(0, len(terms), 2)]
    return terms[0]


def products(rows, bank_ref, j, targets):
    tiles = rows.shape[0] // 16
    both = jnp.concatenate([bank_ref[j], bank_ref[j + 1]], axis=1)
    wide = jnp.dot(rows, both, preferred_element_type=jnp.float32).astype(jnp.bfloat16)
    for h in range(2):
        part = wide[:, 128 * h : 128 * (h + 1)].reshape(tiles, 16, 128)
        for ref, step, at, low, count in targets:
            start = (j + h) * step + at
            ref[start : start + count] = part[low : low + count]


def local_kernel(dims, index_ref, x_ref, near_ref, far_ref, bank_ref, out_ref, *scratch):
    gw, gt, entries, unrolled = dims
    index, held, bank, top, low, total, sem = scratch
    even = lax.rem(lax.axis_index("weld"), 2) == 0
    half, kernels = gw // 2, bank.shape[0]
    step = (half + 2) * gt
    cut = (half + 1) * gt
    part = kernels // 2
    own = held.at[gt : (gw + 1) * gt]
    copies = [
        pltpu.make_async_copy(a, b, sem.at[i])
        for i, (a, b) in enumerate(
            (
                (bank_ref.at[:part], bank.at[:part]),
                (x_ref.at[:cut], own.at[:cut]),
                (near_ref, held.at[pl.ds(pick(even, (gw + 1) * gt, 0), gt)]),
                (far_ref, held.at[pl.ds(pick(even, 0, (gw + 1) * gt), gt)]),
                (bank_ref.at[part:], bank.at[part:]),
                (x_ref.at[cut:], own.at[cut:]),
                (index_ref, index),
            )
        )
    ]
    for copy in copies:
        copy.start()
    blank(top)
    blank(low)
    for copy in copies[:4]:
        copy.wait()

    def rows_of(first, count):
        return held[first * gt : (first + count) * gt].reshape(count * gt * 16, 128)

    def gather(table, r, c):
        terms = [table[index[n * gw + r, c]].astype(jnp.float32) for n in range(entries)]
        total[r * gt + c] = tree(terms).astype(total.dtype)

    upper = [(top, step, 0, 0, step), (low, step, 0, half * gt, 2 * gt)]
    lower = [(low, step, 2 * gt, 0, half * gt)]
    for j in range(0, kernels, 2):
        if j == part:
            copies[4].wait()
        products(rows_of(0, half + 2), bank, j, upper)
    copies[5].wait()
    copies[6].wait()
    cells = [(r, c) for r in range(half) for c in range(gt)]
    share = len(cells) * 2 // kernels
    for j in range(0, kernels, 2):
        products(rows_of(half + 2, half), bank, j, lower)
        if unrolled:
            for r, c in cells[j // 2 * share : (j // 2 + 1) * share]:
                gather(top, r, c)

    def store(first, count, i):
        span = pl.ds(first * gt, count * gt)
        copy = pltpu.make_async_copy(total.at[span], out_ref.at[span], sem.at[i])
        copy.start()
        return copy

    def body(r, _, table):
        for c in range(gt):
            gather(table, r, c)
        return 0

    if not unrolled:
        lax.fori_loop(0, half, functools.partial(body, table=top), 0)
    stores = [store(0, half, 0)]
    for i, first in enumerate(range(half, gw, half // 2)):
        if unrolled:
            for r in range(first, first + half // 2):
                body(r, 0, low)
        else:
            lax.fori_loop(first, first + half // 2, functools.partial(body, table=low), 0)
        stores.append(store(first, half // 2, 1 + i))
    for copy in stores:
        copy.wait()


def finish_kernel(dims, side_ref, wall_index_ref, *refs):
    gw, gt, entries, peers, cap, walls, merged = dims
    own_ref = refs[0]
    count = peers - 1 + (0 if merged else 2)
    got = refs[1 : 1 + count]
    bank_ref, wall_bank_ref, _, rates_ref, walls_ref = refs[1 + count : 6 + count]
    table_ref, wall_table_ref, cols_ref, in_sem, out_sem = refs[6 + count :]
    edges = [(rates_ref.at[:, c], cols_ref.at[e]) for e, c in enumerate((0, gt - 1))]
    fetch = [pltpu.make_async_copy(a, b, in_sem.at[e]) for e, (a, b) in enumerate(edges)]
    store = [pltpu.make_async_copy(b, a, out_sem.at[e]) for e, (a, b) in enumerate(edges)]
    for copy in fetch:
        copy.start()
    depth = gw + 2
    if merged:
        sides = [got[0][cap : cap + depth], got[2][cap : cap + depth]]
    else:
        sides = [got[-2][...], got[-1][...]]
    blank(table_ref)
    blank(wall_table_ref)
    ring = jnp.concatenate(sides, axis=0).reshape(2 * depth * 16, 128)
    for j in range(0, bank_ref.shape[0], 2):
        products(ring, bank_ref, j, [(table_ref, 2 * depth, 0, 0, 2 * depth)])
    slots = peers * cap
    received = jnp.concatenate([own_ref[...]] + [g[:cap] for g in got[: peers - 1]], axis=0)
    received = received.reshape(slots * 16, 128)
    for j in range(0, wall_bank_ref.shape[0], 2):
        products(received, wall_bank_ref, j, [(wall_table_ref, slots, 0, 0, slots)])
    for copy in fetch:
        copy.wait()
    for e, c in enumerate((0, gt - 1)):
        for r in range(gw):
            terms = [
                table_ref[side_ref[n * gw + r, c]].astype(jnp.float32) for n in range(entries)
            ]
            base = cols_ref[e, r].astype(jnp.float32)
            cols_ref[e, r] = (base + tree(terms)).astype(cols_ref.dtype)
        store[e].start()
    for j in range(walls):
        picked = [
            wall_table_ref[wall_index_ref[j, m]].astype(jnp.float32)
            for m in range(wall_index_ref.shape[1])
        ]
        sums = tree(picked)
        walls_ref[j] = (sums / (1.0 + sums[0:1, :])).astype(walls_ref.dtype)
    for copy in store:
        copy.wait()


def pairing(count, shift):
    pairs = []
    for low in range(shift, count - 1, 2):
        pairs += [(low, low + 1), (low + 1, low)]
    return pairs


def on_device(
    features, pair_offsets, pair_kernel, kernels, send_list, wall_slots, wall_kernel, wall_kernels
):
    gw, gt, channels, tile = features.shape
    entries = pair_offsets.shape[2]
    bank, wall_bank = kernels.shape[0], wall_kernels.shape[0]
    peers, cap = send_list.shape[2:]
    walls, picks = wall_slots.shape[2:]
    weld = lax.axis_size("weld")
    merged = peers == 4
    depth = gw + 2
    i32, bf16 = jnp.int32, jnp.bfloat16
    total = gw * gt
    tiles = features.reshape(total, channels, tile)
    lists = send_list.reshape(peers, cap)

    def stack(n):
        return jax.ShapeDtypeStruct((n, channels, tile), bf16)

    def buffer(n):
        return pltpu.VMEM((n, channels, tile), bf16)

    def cost(flops, mib):
        return pl.CostEstimate(flops=flops, bytes_accessed=mib * MIB, transcendentals=0)

    early = (2,) if merged else tuple(range(2, peers))
    late = (1, 3, 0) if merged else (1, 0)
    near_out, far_out, *early_out = pl.pallas_call(
        functools.partial(first_kernel, (gw, gt), early),
        name="edge_rows",
        out_shape=(stack(gt), stack(gt)) + (stack(cap),) * len(early),
        in_specs=[SMEM, HBM],
        out_specs=(HBM, HBM) + (VMEM,) * len(early),
        scratch_shapes=[buffer(total + 1), pltpu.SemaphoreType.DMA((3,))],
        cost_estimate=cost(0, 2),
    )(lists, tiles)
    near = lax.ppermute(near_out, "weld", pairing(weld, 0))
    far = lax.ppermute(far_out, "weld", pairing(weld, 1))
    got = {}
    for k, message in zip(early, early_out):
        got[k] = lax.ppermute(message, "trans", [(i, i ^ k) for i in range(peers)])

    table_index = jax.ShapeDtypeStruct((entries, gw, 128), i32)
    local_index, side_index, wall_index = pl.pallas_call(
        functools.partial(index_kernel, (gw, gt, bank, wall_bank, peers, cap)),
        name="pair_index",
        out_shape=(table_index, table_index, jax.ShapeDtypeStruct((walls, picks), i32)),
        in_specs=[VMEM] * 4,
        out_specs=(VMEM, VMEM, VMEM),
        cost_estimate=cost(1_000_000, 3),
    )(
        pair_offsets.transpose(2, 0, 1),
        pair_kernel.transpose(2, 0, 1),
        wall_slots.reshape(walls, picks),
        wall_kernel.reshape(walls, picks),
    )
    local_index = local_index.reshape(entries * gw, 128)
    side_index = side_index.reshape(entries * gw, 128)

    lengths = [cap + (depth if merged and k else 0) for k in late]
    if not merged:
        lengths += [depth, depth]
    late_out = pl.pallas_call(
        functools.partial(second_kernel, (gw, gt, cap), late, merged),
        name="edge_columns",
        out_shape=tuple(stack(n) for n in lengths),
        in_specs=[SMEM, HBM, HBM, HBM],
        out_specs=(VMEM,) * len(lengths),
        scratch_shapes=[
            buffer(total + 1),
            pltpu.SemaphoreType.DMA,
            pltpu.SemaphoreType.DMA((4,)),
        ],
        compiler_params=pltpu.CompilerParams(vmem_limit_bytes=8 * MIB),
        cost_estimate=cost(0, 2),
    )(lists, tiles, near, far)
    for k, message in zip(late, late_out):
        if k:
            got[k] = lax.ppermute(message, "trans", [(i, i ^ k) for i in range(peers)])
    own = late_out[late.index(0)]
    received = [got[k] for k in range(1, peers)]
    if not merged:
        received += [
            lax.ppermute(late_out[len(late) + s], "trans", pairing(peers, s)) for s in range(2)
        ]

    step = (gw // 2 + 2) * gt
    rates = pl.pallas_call(
        functools.partial(local_kernel, (gw, gt, entries, UNROLLED)),
        name="local_pairs",
        out_shape=stack(total),
        in_specs=[HBM] * 5,
        out_specs=HBM,
        scratch_shapes=[
            pltpu.SMEM((entries * gw, 128), i32),
            buffer((gw + 2) * gt),
            pltpu.VMEM(kernels.shape, bf16),
            buffer(bank * step + 1),
            buffer(bank * step + 1),
            buffer(total),
            pltpu.SemaphoreType.DMA((7,)),
        ],
        compiler_params=pltpu.CompilerParams(vmem_limit_bytes=44 * MIB),
        cost_estimate=cost(2 * (gw + 2) * gt * channels * tile * tile * bank, 30),
    )(local_index, tiles, near, far, kernels)

    count = len(received)
    rates, wall_out = pl.pallas_call(
        functools.partial(finish_kernel, (gw, gt, entries, peers, cap, walls, merged)),
        name="columns_and_walls",
        out_shape=(jax.ShapeDtypeStruct((gw, gt, channels, tile), bf16), stack(walls)),
        in_specs=[SMEM, SMEM] + [VMEM] * (3 + count) + [HBM],
        out_specs=(HBM, VMEM),
        scratch_shapes=[
            buffer(bank * 2 * depth + 1),
            buffer(wall_bank * peers * cap + 1),
            pltpu.VMEM((2, gw, channels, tile), bf16),
            pltpu.SemaphoreType.DMA((2,)),
            pltpu.SemaphoreType.DMA((2,)),
        ],
        input_output_aliases={5 + count: 0},
        compiler_params=pltpu.CompilerParams(vmem_limit_bytes=44 * MIB),
        cost_estimate=cost(2 * peers * cap * channels * tile * tile * wall_bank, 8),
    )(
        side_index,
        wall_index,
        own,
        *received,
        kernels,
        wall_kernels,
        rates.reshape(gw, gt, channels, tile),
    )
    return rates, wall_out.reshape(1, 1, walls, channels, tile)


def solution(mesh):
    in_specs = (
        P("weld", "trans", None, None),
        P("weld", "trans", None),
        P("weld", "trans", None),
        P(),
        P("weld", "trans", None, None),
        P("weld", "trans", None, None),
        P("weld", "trans", None, None),
        P(),
    )
    out_specs = (P("weld", "trans", None, None), P("weld", "trans", None, None, None))
    return jax.shard_map(
        on_device, mesh=mesh, in_specs=in_specs, out_specs=out_specs, check_vma=False
    )
```

profile of v0, /device:TPU:1, one launch (start us, length us, event | category | flops | bytes accessed | tf_op | source)
XLA Modules:
  0.0 41.8 jit_solution(6797180282890192452)
XLA Ops:
  0.6 0.0 copy-start
  0.6 10.6 %edge_rows.1 = (bf16[32,16,128]{2,1,0:T(8,128)(2,1)}, bf16[32,16,128]{2,1,0:T(8,128)(2,1)}, bf16[32,16,128]{2,1,0:T(8,128)(2,1)}) custom-call(s32[4,32]{1,0:T(4,128)} %bitcast.14, bf16[256,16,128]{2,1,0:T(8,128)(2,1)} %bitcast.10), custom_call_target="tpu_custom_call" | custom-call | bytes 2097152 | tf_op jit(solution)/shard_map/edge_rows/pallas_call | solution.py:299
  11.2 0.1 collective-permute-start
  11.3 4.5 %collective-permute-start.1 = (bf16[32,16,128]{2,1,0:T(8,128)(2,1)}, bf16[32,16,128]{2,1,0:T(8,128)(2,1)S(1)}, u32[]{:S(2)}, u32[]{:S(2)}) collective-permute-start(bf16[32,16,128]{2,1,0:T(8,128)(2,1)} %get-tuple-element.16), channel_id=1, source_target_pairs={{4,8},{8,4},{12,16},{16,12},{20,24},{24,20},{5,9},{9,5},{13,17},{1... | collective-permute-start | bytes 393224 | tf_op jit(solution)/shard_map/ppermute | solution.py:309
  15.8 2.4 %collective-permute-start.3 = (bf16[32,16,128]{2,1,0:T(8,128)(2,1)}, bf16[32,16,128]{2,1,0:T(8,128)(2,1)S(1)}, u32[]{:S(2)}, u32[]{:S(2)}) collective-permute-start(bf16[32,16,128]{2,1,0:T(8,128)(2,1)} %get-tuple-element.19), channel_id=1, source_target_pairs={{0,2},{1,3},{2,0},{3,1},{4,6},{5,7},{6,4},{7,5},{8,10},{9,11},{10,... | collective-permute-start | bytes 393224 | tf_op jit(solution)/shard_map/ppermute | solution.py:312
  18.2 0.0 copy-start.5
  18.2 1.5 %pair_index.1 = (s32[12,8,128]{2,1,0:T(8,128)}, s32[12,8,128]{2,1,0:T(8,128)}, s32[16,16]{1,0:T(8,128)}) custom-call(s32[12,8,32]{2,1,0:T(8,128)} %bitcast.18, s32[12,8,32]{2,1,0:T(8,128)} %bitcast.19, s32[16,16]{1,0:T(8,128)} %bitcast.20, s32[16,16]{1,0:T(8,128)} %bitcast.21), custom_call_target="tpu_custom_call" | custom-call | flops 1000000 | bytes 3145728 | tf_op jit(solution)/shard_map/pair_index/pallas_call | solution.py:315
  19.7 0.0 copy-start.1
  19.7 0.0 copy-start.6
  19.7 0.0 collective-permute-done.near_ref
  19.7 0.0 collective-permute-done.1.far_ref
  19.7 0.0 copy-done
  19.7 0.0 copy-done.5
  19.7 0.8 %edge_columns.1 = (bf16[42,16,128]{2,1,0:T(8,128)(2,1)S(1)}, bf16[42,16,128]{2,1,0:T(8,128)(2,1)S(1)}, bf16[32,16,128]{2,1,0:T(8,128)(2,1)S(1)}) custom-call(s32[4,32]{1,0:T(4,128)S(1)} %bitcast.15, bf16[256,16,128]{2,1,0:T(8,128)(2,1)S(1)} %bitcast.11, bf16[32,16,128]{2,1,0:T(8,128)(2,1)S(1)} %collective-permute-done.near_ref, ...), custom_call_target="tpu_custom_call" | custom-call | bytes 2097152 | tf_op jit(solution)/shard_map/edge_columns/pallas_call | solution.py:334
  20.6 2.0 %collective-permute-start.2 = (bf16[42,16,128]{2,1,0:T(8,128)(2,1)S(1)}, bf16[42,16,128]{2,1,0:T(8,128)(2,1)S(1)}, u32[]{:S(2)}, u32[]{:S(2)}) collective-permute-start(bf16[42,16,128]{2,1,0:T(8,128)(2,1)S(1)} %get-tuple-element.18), channel_id=1, source_target_pairs={{0,1},{1,0},{2,3},{3,2},{4,5},{5,4},{6,7},{7,6},{8,9},{9,8},{10,11... | collective-permute-start | bytes 516104 | tf_op jit(solution)/shard_map/ppermute | solution.py:350
  22.6 2.5 %collective-permute-start.4 = (bf16[42,16,128]{2,1,0:T(8,128)(2,1)S(1)}, bf16[42,16,128]{2,1,0:T(8,128)(2,1)S(1)}, u32[]{:S(2)}, u32[]{:S(2)}) collective-permute-start(bf16[42,16,128]{2,1,0:T(8,128)(2,1)S(1)} %get-tuple-element.20), channel_id=1, source_target_pairs={{0,3},{1,2},{2,1},{3,0},{4,7},{5,6},{6,5},{7,4},{8,11},{9,10},{10,... | collective-permute-start | bytes 516104 | tf_op jit(solution)/shard_map/ppermute | solution.py:350
  25.1 0.0 copy-done.1
  25.1 0.0 copy-done.6
  25.1 0.0 copy-start.2
  25.1 0.0 copy-start.3
  25.1 10.9 %local_pairs.1 = bf16[256,16,128]{2,1,0:T(8,128)(2,1)} custom-call(s32[96,128]{1,0:T(8,128)S(1)} %bitcast.16, bf16[256,16,128]{2,1,0:T(8,128)(2,1)S(1)} %bitcast.12, bf16[32,16,128]{2,1,0:T(8,128)(2,1)S(1)} %collective-permute-done.near_ref, bf16[32,16,128]{2,1,0:T(8,128)(2,1)S(1)} %collective-permute-done.1.far_ref, bf16[16,128,128]{2,1,0:T(8,128)(2,1)S(1)} %copy-done.1), custom_call_target="tpu_custom_call" | custom-call | flops 2684354560 | bytes 31457280 | tf_op jit(solution)/shard_map/local_pairs/pallas_call | solution.py:359
  35.9 0.0 copy-start.4
  36.0 0.0 collective-permute-done.3.refs_2_
  36.0 0.0 collective-permute-done.2.refs_1_
  36.0 0.0 collective-permute-done.4.refs_3_
  36.0 0.0 copy-done.2
  36.0 0.0 copy-done.3
  36.0 0.6 %copy-done.4 = s32[16,16]{1,0:T(8,128)S(1)} copy-done((s32[16,16]{1,0:T(8,128)S(1)}, s32[16,16]{1,0:T(8,128)}, u32[]{:S(2)}) %copy-start.4) | copy-done | bytes 1048
  36.6 5.1 %columns_and_walls.1 = (bf16[8,32,16,128]{3,2,1,0:T(8,128)(2,1)}, bf16[16,16,128]{2,1,0:T(8,128)(2,1)}) custom-call(s32[96,128]{1,0:T(8,128)S(1)} %bitcast.13, s32[16,16]{1,0:T(8,128)S(1)} %copy-done.4, bf16[32,16,128]{2,1,0:T(8,128)(2,1)S(1)} %get-tuple-element.17.refs_0_, ...), custom_call_target="tpu_custom_call", output_to_operand_aliasing={{0}: (8, {})} | custom-call | flops 536870912 | bytes 8388608 | tf_op jit(solution)/shard_map/columns_and_walls/pallas_call | solution.py:379
Async XLA Ops:
  0.6 19.1 %copy-start = (bf16[8,32,16,128]{3,2,1,0:T(8,128)(2,1)S(1)}, bf16[8,32,16,128]{3,2,1,0:T(8,128)(2,1)}, u32[]{:S(2)}) copy-start(bf16[8,32,16,128]{3,2,1,0:T(8,128)(2,1)} %param.8) | copy-start | bytes 3145732
  11.2 8.5 %collective-permute-start = (bf16[32,16,128]{2,1,0:T(8,128)(2,1)}, bf16[32,16,128]{2,1,0:T(8,128)(2,1)S(1)}, u32[]{:S(2)}, u32[]{:S(2)}) collective-permute-start(bf16[32,16,128]{2,1,0:T(8,128)(2,1)} %get-tuple-element.15), channel_id=1, source_target_pairs={{0,4},{4,0},{8,12},{12,8},{16,20},{20,16},{24,28},{28,24},{1,5},{5... | collective-permute-start | bytes 393224 | tf_op jit(solution)/shard_map/ppermute | solution.py:308
  11.3 8.4 %collective-permute-start.1 = (bf16[32,16,128]{2,1,0:T(8,128)(2,1)}, bf16[32,16,128]{2,1,0:T(8,128)(2,1)S(1)}, u32[]{:S(2)}, u32[]{:S(2)}) collective-permute-start(bf16[32,16,128]{2,1,0:T(8,128)(2,1)} %get-tuple-element.16), channel_id=1, source_target_pairs={{4,8},{8,4},{12,16},{16,12},{20,24},{24,20},{5,9},{9,5},{13,17},{1... | collective-permute-start | bytes 393224 | tf_op jit(solution)/shard_map/ppermute | solution.py:309
  15.8 20.2 %collective-permute-start.3 = (bf16[32,16,128]{2,1,0:T(8,128)(2,1)}, bf16[32,16,128]{2,1,0:T(8,128)(2,1)S(1)}, u32[]{:S(2)}, u32[]{:S(2)}) collective-permute-start(bf16[32,16,128]{2,1,0:T(8,128)(2,1)} %get-tuple-element.19), channel_id=1, source_target_pairs={{0,2},{1,3},{2,0},{3,1},{4,6},{5,7},{6,4},{7,5},{8,10},{9,11},{10,... | collective-permute-start | bytes 393224 | tf_op jit(solution)/shard_map/ppermute | solution.py:312
  18.2 1.6 %copy-start.5 = (s32[1,1,4,32]{3,2,1,0:T(4,128)S(1)}, s32[1,1,4,32]{3,2,1,0:T(4,128)}, u32[]{:S(2)}) copy-start(s32[1,1,4,32]{3,2,1,0:T(4,128)} %param.12) | copy-start | bytes 1540
  19.7 5.4 %copy-start.1 = (bf16[16,128,128]{2,1,0:T(8,128)(2,1)S(1)}, bf16[16,128,128]{2,1,0:T(8,128)(2,1)}, u32[]{:S(2)}) copy-start(bf16[16,128,128]{2,1,0:T(8,128)(2,1)} %refs_4_.1) | copy-start | bytes 1572868
  19.7 5.4 %copy-start.6 = (s32[12,8,128]{2,1,0:T(8,128)S(1)}, s32[12,8,128]{2,1,0:T(8,128)}, u32[]{:S(2)}) copy-start(s32[12,8,128]{2,1,0:T(8,128)} %get-tuple-element.21) | copy-start | bytes 147460
  20.6 15.4 %collective-permute-start.2 = (bf16[42,16,128]{2,1,0:T(8,128)(2,1)S(1)}, bf16[42,16,128]{2,1,0:T(8,128)(2,1)S(1)}, u32[]{:S(2)}, u32[]{:S(2)}) collective-permute-start(bf16[42,16,128]{2,1,0:T(8,128)(2,1)S(1)} %get-tuple-element.18), channel_id=1, source_target_pairs={{0,1},{1,0},{2,3},{3,2},{4,5},{5,4},{6,7},{7,6},{8,9},{9,8},{10,11... | collective-permute-start | bytes 516104 | tf_op jit(solution)/shard_map/ppermute | solution.py:350
  22.6 13.4 %collective-permute-start.4 = (bf16[42,16,128]{2,1,0:T(8,128)(2,1)S(1)}, bf16[42,16,128]{2,1,0:T(8,128)(2,1)S(1)}, u32[]{:S(2)}, u32[]{:S(2)}) collective-permute-start(bf16[42,16,128]{2,1,0:T(8,128)(2,1)S(1)} %get-tuple-element.20), channel_id=1, source_target_pairs={{0,3},{1,2},{2,1},{3,0},{4,7},{5,6},{6,5},{7,4},{8,11},{9,10},{10,... | collective-permute-start | bytes 516104 | tf_op jit(solution)/shard_map/ppermute | solution.py:350
  25.1 10.9 %copy-start.2 = (bf16[8,128,128]{2,1,0:T(8,128)(2,1)S(1)}, bf16[8,128,128]{2,1,0:T(8,128)(2,1)}, u32[]{:S(2)}) copy-start(bf16[8,128,128]{2,1,0:T(8,128)(2,1)} %refs_5_.1) | copy-start | bytes 786436
  25.1 10.9 %copy-start.3 = (s32[12,8,128]{2,1,0:T(8,128)S(1)}, s32[12,8,128]{2,1,0:T(8,128)}, u32[]{:S(2)}) copy-start(s32[12,8,128]{2,1,0:T(8,128)} %get-tuple-element.13) | copy-start | bytes 147460
  35.9 0.7 %copy-start.4 = (s32[16,16]{1,0:T(8,128)S(1)}, s32[16,16]{1,0:T(8,128)}, u32[]{:S(2)}) copy-start(s32[16,16]{1,0:T(8,128)} %get-tuple-element.14.wall_index_ref) | copy-start | bytes 3076
where the time goes:
time: 42.1 us; the launch traced here: 41.8 us
  Pallas kernels  28.9 us (69%)
  starting transfers between devices  11.4 us (27%)
  between operations  0.75 us (2%)
  local copies, waits for them, and re-layouts  0.66 us (2%)
    pallas_call x1, Pallas kernels, on_device(): pl.pallas_call(functools.partial(local_kernel, (gw, gt, entries, UNROLLED...  10.9 us
    pallas_call x1, Pallas kernels, on_device(): pl.pallas_call(functools.partial(first_kernel, (gw, gt), early), name='ed...  10.6 us
    ppermute x3, starting transfers between devices, on_device(): got[k] = lax.ppermute(message, 'trans', [(i, i ^ k) for i in range(peers)])  6.85 us
    pallas_call x1, Pallas kernels, on_device(): pl.pallas_call(functools.partial(finish_kernel, (gw, gt, entries, peers,...  5.15 us
    ppermute x1, starting transfers between devices, on_device(): far = lax.ppermute(far_out, 'weld', pairing(weld, 1))  4.46 us
    pallas_call x1, Pallas kernels, on_device(): pl.pallas_call(functools.partial(index_kernel, (gw, gt, bank, wall_bank,...  1.53 us
  transfers between devices with their start and end apart: 5, of which 0 were waited for; matrix products, arithmetic and copies ran while one was open for 0% of the time, Pallas kernels for 32%

commit v1 on v0

--- a/solution.py
+++ b/solution.py
@@ -12,13 +12,14 @@
 HBM = pl.BlockSpec(memory_space=pl.ANY)
 MIB = 1 << 20
 UNROLLED = False
+WALL_LANE = 64
 
 
 def pick(cond, a, b):
     return lax.select(cond, jnp.int32(a), jnp.int32(b))
 
 
-def index_kernel(dims, off_ref, kind_ref, slot_ref, wkind_ref, local_ref, side_ref, wall_ref):
+def index_kernel(dims, off_ref, kind_ref, slot_ref, wkind_ref, local_ref, side_ref):
     gw, gt, bank, wall_bank, peers, cap = dims
     t = lax.axis_index("trans")
     off, kind = off_ref[...], kind_ref[...]
@@ -41,11 +42,13 @@
     )
     slot = slot_ref[...]
     sender = slot // cap
-    wall_ref[...] = jnp.where(
+    wall = jnp.where(
         slot >= peers * cap,
         wall_bank * peers * cap,
         wkind_ref[...] * (peers * cap) + (sender ^ t) * cap + (slot - sender * cap),
     )
+    for q in range(slot.shape[0] // gw):
+        side_ref[q, :, WALL_LANE : WALL_LANE + slot.shape[1]] = wall[q * gw : (q + 1) * gw]
 
 
 def load_tiles(x_ref, held_ref, sem):
@@ -67,18 +70,28 @@
     outs, (held_ref, sem) = refs[: len(early)], refs[len(early) :]
     w, t = lax.axis_index("weld"), lax.axis_index("trans")
     even = lax.rem(w, 2) == 0
-    load = load_tiles(x_ref, held_ref, sem.at[0])
-    load.start()
-    rows = []
-    for i, (ref, row) in enumerate(
-        ((near_ref, pick(even, gw - 1, 0)), (far_ref, pick(even, 0, gw - 1)))
-    ):
-        rows.append(
-            pltpu.make_async_copy(x_ref.at[pl.ds(row * gt, gt)], ref, sem.at[1 + i])
+
+    def span(first, count):
+        return pl.ds(first * gt, count * gt)
+
+    loads = [
+        pltpu.make_async_copy(x_ref.at[at], held_ref.at[at], sem.at[i])
+        for i, at in enumerate((span(0, 1), span(gw - 1, 1), span(1, gw - 2)))
+    ]
+    for copy in loads:
+        copy.start()
+    blank(held_ref)
+    loads[0].wait()
+    loads[1].wait()
+    rows = [
+        pltpu.make_async_copy(held_ref.at[span(row, 1)], ref, sem.at[3 + i])
+        for i, (ref, row) in enumerate(
+            ((near_ref, pick(even, gw - 1, 0)), (far_ref, pick(even, 0, gw - 1)))
         )
-        rows[i].start()
-    blank(held_ref)
-    load.wait()
+    ]
+    for copy in rows:
+        copy.start()
+    loads[2].wait()
     for k, ref in zip(early, outs):
         listed(held_ref, list_ref, t ^ k, ref)
     for copy in rows:
@@ -136,38 +149,18 @@
             ref[start : start + count] = part[low : low + count]
 
 
-def local_kernel(dims, index_ref, x_ref, near_ref, far_ref, bank_ref, out_ref, *scratch):
+def local_kernel(dims, index_ref, x_ref, near_ref, far_ref, bank, out_ref, *scratch):
     gw, gt, entries, unrolled = dims
-    index, held, bank, top, low, total, sem = scratch
+    index, top, low, total, index_sem, sem = scratch
     even = lax.rem(lax.axis_index("weld"), 2) == 0
     half, kernels = gw // 2, bank.shape[0]
     step = (half + 2) * gt
-    cut = (half + 1) * gt
-    part = kernels // 2
-    own = held.at[gt : (gw + 1) * gt]
-    copies = [
-        pltpu.make_async_copy(a, b, sem.at[i])
-        for i, (a, b) in enumerate(
-            (
-                (bank_ref.at[:part], bank.at[:part]),
-                (x_ref.at[:cut], own.at[:cut]),
-                (near_ref, held.at[pl.ds(pick(even, (gw + 1) * gt, 0), gt)]),
-                (far_ref, held.at[pl.ds(pick(even, 0, (gw + 1) * gt), gt)]),
-                (bank_ref.at[part:], bank.at[part:]),
-                (x_ref.at[cut:], own.at[cut:]),
-                (index_ref, index),
-            )
-        )
-    ]
-    for copy in copies:
-        copy.start()
+    fetch = pltpu.make_async_copy(index_ref, index, index_sem)
+    fetch.start()
     blank(top)
     blank(low)
-    for copy in copies[:4]:
-        copy.wait()
-
-    def rows_of(first, count):
-        return held[first * gt : (first + count) * gt].reshape(count * gt * 16, 128)
+    before = jnp.where(even, far_ref[...], near_ref[...])
+    after = jnp.where(even, near_ref[...], far_ref[...])
 
     def gather(table, r, c):
         terms = [table[index[n * gw + r, c]].astype(jnp.float32) for n in range(entries)]
@@ -175,16 +168,16 @@
 
     upper = [(top, step, 0, 0, step), (low, step, 0, half * gt, 2 * gt)]
     lower = [(low, step, 2 * gt, 0, half * gt)]
+    cut = (half + 1) * gt
+    first = jnp.concatenate([before, x_ref[:cut]], axis=0).reshape(step * 16, 128)
     for j in range(0, kernels, 2):
-        if j == part:
-            copies[4].wait()
-        products(rows_of(0, half + 2), bank, j, upper)
-    copies[5].wait()
-    copies[6].wait()
+        products(first, bank, j, upper)
+    fetch.wait()
+    second = jnp.concatenate([x_ref[cut:], after], axis=0).reshape(half * gt * 16, 128)
     cells = [(r, c) for r in range(half) for c in range(gt)]
     share = len(cells) * 2 // kernels
     for j in range(0, kernels, 2):
-        products(rows_of(half + 2, half), bank, j, lower)
+        products(second, bank, j, lower)
         if unrolled:
             for r, c in cells[j // 2 * share : (j // 2 + 1) * share]:
                 gather(top, r, c)
@@ -214,16 +207,17 @@
         copy.wait()
 
 
-def finish_kernel(dims, side_ref, wall_index_ref, *refs):
-    gw, gt, entries, peers, cap, walls, merged = dims
+def finish_kernel(dims, side_hbm, *refs):
+    gw, gt, entries, peers, cap, walls, picks, merged = dims
     own_ref = refs[0]
     count = peers - 1 + (0 if merged else 2)
     got = refs[1 : 1 + count]
     bank_ref, wall_bank_ref, _, rates_ref, walls_ref = refs[1 + count : 6 + count]
-    table_ref, wall_table_ref, cols_ref, in_sem, out_sem = refs[6 + count :]
+    side_ref, table_ref, wall_table_ref, cols_ref, in_sem, out_sem = refs[6 + count :]
     edges = [(rates_ref.at[:, c], cols_ref.at[e]) for e, c in enumerate((0, gt - 1))]
     fetch = [pltpu.make_async_copy(a, b, in_sem.at[e]) for e, (a, b) in enumerate(edges)]
     store = [pltpu.make_async_copy(b, a, out_sem.at[e]) for e, (a, b) in enumerate(edges)]
+    fetch.append(pltpu.make_async_copy(side_hbm, side_ref, in_sem.at[2]))
     for copy in fetch:
         copy.start()
     depth = gw + 2
@@ -253,8 +247,7 @@
         store[e].start()
     for j in range(walls):
         picked = [
-            wall_table_ref[wall_index_ref[j, m]].astype(jnp.float32)
-            for m in range(wall_index_ref.shape[1])
+            wall_table_ref[side_ref[j, WALL_LANE + m]].astype(jnp.float32) for m in range(picks)
         ]
         sums = tree(picked)
         walls_ref[j] = (sums / (1.0 + sums[0:1, :])).astype(walls_ref.dtype)
@@ -302,7 +295,7 @@
         out_shape=(stack(gt), stack(gt)) + (stack(cap),) * len(early),
         in_specs=[SMEM, HBM],
         out_specs=(HBM, HBM) + (VMEM,) * len(early),
-        scratch_shapes=[buffer(total + 1), pltpu.SemaphoreType.DMA((3,))],
+        scratch_shapes=[buffer(total + 1), pltpu.SemaphoreType.DMA((5,))],
         cost_estimate=cost(0, 2),
     )(lists, tiles)
     near = lax.ppermute(near_out, "weld", pairing(weld, 0))
@@ -312,12 +305,12 @@
         got[k] = lax.ppermute(message, "trans", [(i, i ^ k) for i in range(peers)])
 
     table_index = jax.ShapeDtypeStruct((entries, gw, 128), i32)
-    local_index, side_index, wall_index = pl.pallas_call(
+    local_index, side_index = pl.pallas_call(
         functools.partial(index_kernel, (gw, gt, bank, wall_bank, peers, cap)),
         name="pair_index",
-        out_shape=(table_index, table_index, jax.ShapeDtypeStruct((walls, picks), i32)),
+        out_shape=(table_index, table_index),
         in_specs=[VMEM] * 4,
-        out_specs=(VMEM, VMEM, VMEM),
+        out_specs=(VMEM, VMEM),
         cost_estimate=cost(1_000_000, 3),
     )(
         pair_offsets.transpose(2, 0, 1),
@@ -360,16 +353,15 @@
         functools.partial(local_kernel, (gw, gt, entries, UNROLLED)),
         name="local_pairs",
         out_shape=stack(total),
-        in_specs=[HBM] * 5,
+        in_specs=[HBM] + [VMEM] * 4,
         out_specs=HBM,
         scratch_shapes=[
             pltpu.SMEM((entries * gw, 128), i32),
-            buffer((gw + 2) * gt),
-            pltpu.VMEM(kernels.shape, bf16),
             buffer(bank * step + 1),
             buffer(bank * step + 1),
             buffer(total),
-            pltpu.SemaphoreType.DMA((7,)),
+            pltpu.SemaphoreType.DMA,
+            pltpu.SemaphoreType.DMA((3,)),
         ],
         compiler_params=pltpu.CompilerParams(vmem_limit_bytes=44 * MIB),
         cost_estimate=cost(2 * (gw + 2) * gt * channels * tile * tile * bank, 30),
@@ -377,24 +369,24 @@
 
     count = len(received)
     rates, wall_out = pl.pallas_call(
-        functools.partial(finish_kernel, (gw, gt, entries, peers, cap, walls, merged)),
+        functools.partial(finish_kernel, (gw, gt, entries, peers, cap, walls, picks, merged)),
         name="columns_and_walls",
         out_shape=(jax.ShapeDtypeStruct((gw, gt, channels, tile), bf16), stack(walls)),
-        in_specs=[SMEM, SMEM] + [VMEM] * (3 + count) + [HBM],
+        in_specs=[HBM] + [VMEM] * (3 + count) + [HBM],
         out_specs=(HBM, VMEM),
         scratch_shapes=[
+            pltpu.SMEM((entries * gw, 128), i32),
             buffer(bank * 2 * depth + 1),
             buffer(wall_bank * peers * cap + 1),
             pltpu.VMEM((2, gw, channels, tile), bf16),
-            pltpu.SemaphoreType.DMA((2,)),
+            pltpu.SemaphoreType.DMA((3,)),
             pltpu.SemaphoreType.DMA((2,)),
         ],
-        input_output_aliases={5 + count: 0},
+        input_output_aliases={4 + count: 0},
         compiler_params=pltpu.CompilerParams(vmem_limit_bytes=44 * MIB),
         cost_estimate=cost(2 * peers * cap * channels * tile * tile * wall_bank, 8),
     )(
         side_index,
-        wall_index,
         own,
         *received,
         kernels,

time: 42.1 us -> 32.2 us (0.76)
  Pallas kernels: 28.9 us -> 19.7 us
  local copies, waits for them, and re-layouts: 0.66 us -> 0.02 us
    pallas_call x1, Pallas kernels: 10.6 us -> 3.18 us  [on_device(): pl.pallas_call(functools.partial(first_kernel, (gw, gt), early), name='ed...]
    pallas_call x1, Pallas kernels: 10.9 us -> 9.91 us  [on_device(): pl.pallas_call(functools.partial(local_kernel, (gw, gt, entries, UNROLLED...]
    pallas_call x1, Pallas kernels: 5.15 us -> 4.27 us  [on_device(): pl.pallas_call(functools.partial(finish_kernel, (gw, gt, entries, peers,...]
    unnamed x14 -> x12, local copies, waits for them, and re-layouts: 0.66 us -> 0.02 us
  transfers between devices with their start and end apart: 5 -> 5, of which waited for: 0 -> 0; matrix products, arithmetic and copies ran while one was open for 0% -> 0% of each run, Pallas kernels for 32% -> 38%
where the time goes in v1:
time: 32.2 us; the launch traced here: 31.9 us
  Pallas kernels  19.7 us (61%)
  starting transfers between devices  11.4 us (35%)
  between operations  0.74 us (2%)
    pallas_call x1, Pallas kernels, on_device(): pl.pallas_call(functools.partial(local_kernel, (gw, gt, entries, UNROLLED...  9.91 us
    ppermute x3, starting transfers between devices, on_device(): got[k] = lax.ppermute(message, 'trans', [(i, i ^ k) for i in range(peers)])  6.84 us
    ppermute x1, starting transfers between devices, on_device(): far = lax.ppermute(far_out, 'weld', pairing(weld, 1))  4.46 us
    pallas_call x1, Pallas kernels, on_device(): pl.pallas_call(functools.partial(finish_kernel, (gw, gt, entries, peers,...  4.27 us
    pallas_call x1, Pallas kernels, on_device(): pl.pallas_call(functools.partial(first_kernel, (gw, gt), early), name='ed...  3.18 us
    pallas_call x1, Pallas kernels, on_device(): pl.pallas_call(functools.partial(index_kernel, (gw, gt, bank, wall_bank,...  1.54 us
    pallas_call x1, Pallas kernels, on_device(): pl.pallas_call(functools.partial(second_kernel, (gw, gt, cap), late, merg...  0.84 us
  transfers between devices with their start and end apart: 5, of which 0 were waited for; matrix products, arithmetic and copies ran while one was open for 0% of the time, Pallas kernels for 38%

profile of v1, /device:TPU:1, one launch (start us, length us, event | category | flops | bytes accessed | tf_op | source)
XLA Modules:
  0.0 31.9 jit_solution(8348692436103837092)
XLA Ops:
  0.6 0.0 copy-start
  0.6 3.2 %edge_rows.1 = (bf16[32,16,128]{2,1,0:T(8,128)(2,1)}, bf16[32,16,128]{2,1,0:T(8,128)(2,1)}, bf16[32,16,128]{2,1,0:T(8,128)(2,1)}) custom-call(s32[4,32]{1,0:T(4,128)} %bitcast.14, bf16[256,16,128]{2,1,0:T(8,128)(2,1)} %bitcast.10), custom_call_target="tpu_custom_call" | custom-call | bytes 2097152 | tf_op jit(solution)/shard_map/edge_rows/pallas_call | solution.py:292
  3.8 0.1 collective-permute-start
  3.9 4.5 %collective-permute-start.1 = (bf16[32,16,128]{2,1,0:T(8,128)(2,1)}, bf16[32,16,128]{2,1,0:T(8,128)(2,1)S(1)}, u32[]{:S(2)}, u32[]{:S(2)}) collective-permute-start(bf16[32,16,128]{2,1,0:T(8,128)(2,1)} %get-tuple-element.14), channel_id=1, source_target_pairs={{4,8},{8,4},{12,16},{16,12},{20,24},{24,20},{5,9},{9,5},{13,17},{1... | collective-permute-start | bytes 393224 | tf_op jit(solution)/shard_map/ppermute | solution.py:302
  8.4 2.4 %collective-permute-start.3 = (bf16[32,16,128]{2,1,0:T(8,128)(2,1)}, bf16[32,16,128]{2,1,0:T(8,128)(2,1)S(1)}, u32[]{:S(2)}, u32[]{:S(2)}) collective-permute-start(bf16[32,16,128]{2,1,0:T(8,128)(2,1)} %get-tuple-element.17), channel_id=1, source_target_pairs={{0,2},{1,3},{2,0},{3,1},{4,6},{5,7},{6,4},{7,5},{8,10},{9,11},{10,... | collective-permute-start | bytes 393224 | tf_op jit(solution)/shard_map/ppermute | solution.py:305
  10.8 0.0 copy-start.4
  10.8 1.5 %pair_index.1 = (s32[12,8,128]{2,1,0:T(8,128)}, s32[12,8,128]{2,1,0:T(8,128)}) custom-call(s32[12,8,32]{2,1,0:T(8,128)} %bitcast.18, s32[12,8,32]{2,1,0:T(8,128)} %bitcast.19, s32[16,16]{1,0:T(8,128)} %bitcast.20, s32[16,16]{1,0:T(8,128)} %bitcast.21), custom_call_target="tpu_custom_call" | custom-call | flops 1000000 | bytes 3145728 | tf_op jit(solution)/shard_map/pair_index/pallas_call | solution.py:308
  12.3 0.0 copy-start.1
  12.3 0.0 copy-start.5
  12.3 0.0 collective-permute-done.near_ref
  12.3 0.0 collective-permute-done.1.far_ref
  12.4 0.0 copy-done
  12.4 0.0 copy-done.4
  12.4 0.8 %edge_columns.1 = (bf16[42,16,128]{2,1,0:T(8,128)(2,1)S(1)}, bf16[42,16,128]{2,1,0:T(8,128)(2,1)S(1)}, bf16[32,16,128]{2,1,0:T(8,128)(2,1)S(1)}) custom-call(s32[4,32]{1,0:T(4,128)S(1)} %bitcast.15, bf16[256,16,128]{2,1,0:T(8,128)(2,1)S(1)} %bitcast.11, bf16[32,16,128]{2,1,0:T(8,128)(2,1)S(1)} %collective-permute-done.near_ref, ...), custom_call_target="tpu_custom_call" | custom-call | bytes 2097152 | tf_op jit(solution)/shard_map/edge_columns/pallas_call | solution.py:327
  13.2 2.0 %collective-permute-start.2 = (bf16[42,16,128]{2,1,0:T(8,128)(2,1)S(1)}, bf16[42,16,128]{2,1,0:T(8,128)(2,1)S(1)}, u32[]{:S(2)}, u32[]{:S(2)}) collective-permute-start(bf16[42,16,128]{2,1,0:T(8,128)(2,1)S(1)} %get-tuple-element.16), channel_id=1, source_target_pairs={{0,1},{1,0},{2,3},{3,2},{4,5},{5,4},{6,7},{7,6},{8,9},{9,8},{10,11... | collective-permute-start | bytes 516104 | tf_op jit(solution)/shard_map/ppermute | solution.py:343
  15.2 2.5 %collective-permute-start.4 = (bf16[42,16,128]{2,1,0:T(8,128)(2,1)S(1)}, bf16[42,16,128]{2,1,0:T(8,128)(2,1)S(1)}, u32[]{:S(2)}, u32[]{:S(2)}) collective-permute-start(bf16[42,16,128]{2,1,0:T(8,128)(2,1)S(1)} %get-tuple-element.18), channel_id=1, source_target_pairs={{0,3},{1,2},{2,1},{3,0},{4,7},{5,6},{6,5},{7,4},{8,11},{9,10},{10,... | collective-permute-start | bytes 516104 | tf_op jit(solution)/shard_map/ppermute | solution.py:343
  17.7 0.0 copy-done.1
  17.7 0.0 copy-done.5
  17.7 0.0 copy-start.2
  17.7 0.0 copy-start.3
  17.7 9.9 %local_pairs.1 = bf16[256,16,128]{2,1,0:T(8,128)(2,1)} custom-call(s32[96,128]{1,0:T(8,128)S(1)} %bitcast.16, bf16[256,16,128]{2,1,0:T(8,128)(2,1)S(1)} %bitcast.12, bf16[32,16,128]{2,1,0:T(8,128)(2,1)S(1)} %collective-permute-done.near_ref, bf16[32,16,128]{2,1,0:T(8,128)(2,1)S(1)} %collective-permute-done.1.far_ref, bf16[16,128,128]{2,1,0:T(8,128)(2,1)S(1)} %copy-done.1), custom_call_target="tpu_custom_call" | custom-call | flops 2684354560 | bytes 31457280 | tf_op jit(solution)/shard_map/local_pairs/pallas_call | solution.py:352
  27.6 0.0 collective-permute-done.3.refs_2_
  27.6 0.0 collective-permute-done.2.refs_1_
  27.6 0.0 collective-permute-done.4.refs_3_
  27.6 0.0 copy-done.2
  27.7 0.0 copy-done.3
  27.7 4.3 %columns_and_walls.1 = (bf16[8,32,16,128]{3,2,1,0:T(8,128)(2,1)}, bf16[16,16,128]{2,1,0:T(8,128)(2,1)}) custom-call(s32[96,128]{1,0:T(8,128)S(1)} %bitcast.13, bf16[32,16,128]{2,1,0:T(8,128)(2,1)S(1)} %get-tuple-element.15.refs_0_, bf16[42,16,128]{2,1,0:T(8,128)(2,1)S(1)} %collective-permute-done.2.refs_1_, ...), custom_call_target="tpu_custom_call", output_to_operand_aliasing={{0}: (7, {})} | custom-call | flops 536870912 | bytes 8388608 | tf_op jit(solution)/shard_map/columns_and_walls/pallas_call | solution.py:371
Async XLA Ops:
  0.6 11.7 %copy-start = (bf16[8,32,16,128]{3,2,1,0:T(8,128)(2,1)S(1)}, bf16[8,32,16,128]{3,2,1,0:T(8,128)(2,1)}, u32[]{:S(2)}) copy-start(bf16[8,32,16,128]{3,2,1,0:T(8,128)(2,1)} %param.8) | copy-start | bytes 3145732
  3.8 8.5 %collective-permute-start = (bf16[32,16,128]{2,1,0:T(8,128)(2,1)}, bf16[32,16,128]{2,1,0:T(8,128)(2,1)S(1)}, u32[]{:S(2)}, u32[]{:S(2)}) collective-permute-start(bf16[32,16,128]{2,1,0:T(8,128)(2,1)} %get-tuple-element.13), channel_id=1, source_target_pairs={{0,4},{4,0},{8,12},{12,8},{16,20},{20,16},{24,28},{28,24},{1,5},{5... | collective-permute-start | bytes 393224 | tf_op jit(solution)/shard_map/ppermute | solution.py:301
  3.9 8.4 %collective-permute-start.1 = (bf16[32,16,128]{2,1,0:T(8,128)(2,1)}, bf16[32,16,128]{2,1,0:T(8,128)(2,1)S(1)}, u32[]{:S(2)}, u32[]{:S(2)}) collective-permute-start(bf16[32,16,128]{2,1,0:T(8,128)(2,1)} %get-tuple-element.14), channel_id=1, source_target_pairs={{4,8},{8,4},{12,16},{16,12},{20,24},{24,20},{5,9},{9,5},{13,17},{1... | collective-permute-start | bytes 393224 | tf_op jit(solution)/shard_map/ppermute | solution.py:302
  8.4 19.2 %collective-permute-start.3 = (bf16[32,16,128]{2,1,0:T(8,128)(2,1)}, bf16[32,16,128]{2,1,0:T(8,128)(2,1)S(1)}, u32[]{:S(2)}, u32[]{:S(2)}) collective-permute-start(bf16[32,16,128]{2,1,0:T(8,128)(2,1)} %get-tuple-element.17), channel_id=1, source_target_pairs={{0,2},{1,3},{2,0},{3,1},{4,6},{5,7},{6,4},{7,5},{8,10},{9,11},{10,... | collective-permute-start | bytes 393224 | tf_op jit(solution)/shard_map/ppermute | solution.py:305
  10.8 1.6 %copy-start.4 = (s32[1,1,4,32]{3,2,1,0:T(4,128)S(1)}, s32[1,1,4,32]{3,2,1,0:T(4,128)}, u32[]{:S(2)}) copy-start(s32[1,1,4,32]{3,2,1,0:T(4,128)} %param.12) | copy-start | bytes 1540
  12.3 5.4 %copy-start.1 = (bf16[16,128,128]{2,1,0:T(8,128)(2,1)S(1)}, bf16[16,128,128]{2,1,0:T(8,128)(2,1)}, u32[]{:S(2)}) copy-start(bf16[16,128,128]{2,1,0:T(8,128)(2,1)} %refs_4_.1) | copy-start | bytes 1572868
  12.3 5.4 %copy-start.5 = (s32[12,8,128]{2,1,0:T(8,128)S(1)}, s32[12,8,128]{2,1,0:T(8,128)}, u32[]{:S(2)}) copy-start(s32[12,8,128]{2,1,0:T(8,128)} %get-tuple-element.19) | copy-start | bytes 147460
  13.2 14.4 %collective-permute-start.2 = (bf16[42,16,128]{2,1,0:T(8,128)(2,1)S(1)}, bf16[42,16,128]{2,1,0:T(8,128)(2,1)S(1)}, u32[]{:S(2)}, u32[]{:S(2)}) collective-permute-start(bf16[42,16,128]{2,1,0:T(8,128)(2,1)S(1)} %get-tuple-element.16), channel_id=1, source_target_pairs={{0,1},{1,0},{2,3},{3,2},{4,5},{5,4},{6,7},{7,6},{8,9},{9,8},{10,11... | collective-permute-start | bytes 516104 | tf_op jit(solution)/shard_map/ppermute | solution.py:343
  15.2 12.4 %collective-permute-start.4 = (bf16[42,16,128]{2,1,0:T(8,128)(2,1)S(1)}, bf16[42,16,128]{2,1,0:T(8,128)(2,1)S(1)}, u32[]{:S(2)}, u32[]{:S(2)}) collective-permute-start(bf16[42,16,128]{2,1,0:T(8,128)(2,1)S(1)} %get-tuple-element.18), channel_id=1, source_target_pairs={{0,3},{1,2},{2,1},{3,0},{4,7},{5,6},{6,5},{7,4},{8,11},{9,10},{10,... | collective-permute-start | bytes 516104 | tf_op jit(solution)/shard_map/ppermute | solution.py:343
  17.7 10.0 %copy-start.2 = (bf16[8,128,128]{2,1,0:T(8,128)(2,1)S(1)}, bf16[8,128,128]{2,1,0:T(8,128)(2,1)}, u32[]{:S(2)}) copy-start(bf16[8,128,128]{2,1,0:T(8,128)(2,1)} %refs_5_.1) | copy-start | bytes 786436
  17.7 10.0 %copy-start.3 = (s32[12,8,128]{2,1,0:T(8,128)S(1)}, s32[12,8,128]{2,1,0:T(8,128)}, u32[]{:S(2)}) copy-start(s32[12,8,128]{2,1,0:T(8,128)} %get-tuple-element.12) | copy-start | bytes 147460

commit v2 on v1

--- a/solution.py
+++ b/solution.py
@@ -11,7 +11,7 @@
 VMEM = pl.BlockSpec(memory_space=pltpu.VMEM)
 HBM = pl.BlockSpec(memory_space=pl.ANY)
 MIB = 1 << 20
-UNROLLED = False
+UNROLLED = True
 WALL_LANE = 64
 
 
@@ -51,23 +51,21 @@
         side_ref[q, :, WALL_LANE : WALL_LANE + slot.shape[1]] = wall[q * gw : (q + 1) * gw]
 
 
-def load_tiles(x_ref, held_ref, sem):
-    count = x_ref.shape[0]
-    return pltpu.make_async_copy(x_ref, held_ref.at[:count], sem)
-
-
 def blank(ref):
     ref[ref.shape[0] - 1] = jnp.zeros(ref.shape[1:], ref.dtype)
 
 
-def listed(held_ref, list_ref, owner, out_ref):
+def listed(held_ref, count, list_ref, owner, out_ref):
+    empty = jnp.zeros(held_ref.shape[1:], held_ref.dtype)
     for c in range(list_ref.shape[1]):
-        out_ref[c] = held_ref[list_ref[owner, c]]
+        item = list_ref[owner, c]
+        tile = held_ref[jnp.minimum(item, count - 1)]
+        out_ref[c] = jnp.where(item < count, tile, empty)
 
 
 def first_kernel(dims, early, list_ref, x_ref, near_ref, far_ref, *refs):
     gw, gt = dims
-    outs, (held_ref, sem) = refs[: len(early)], refs[len(early) :]
+    outs, (picks_ref, held_ref, sem) = refs[: len(early)], refs[len(early) :]
     w, t = lax.axis_index("weld"), lax.axis_index("trans")
     even = lax.rem(w, 2) == 0
 
@@ -78,34 +76,22 @@
         pltpu.make_async_copy(x_ref.at[at], held_ref.at[at], sem.at[i])
         for i, at in enumerate((span(0, 1), span(gw - 1, 1), span(1, gw - 2)))
     ]
+    loads.append(pltpu.make_async_copy(list_ref, picks_ref, sem.at[5]))
     for copy in loads:
         copy.start()
-    blank(held_ref)
     loads[0].wait()
     loads[1].wait()
-    rows = [
-        pltpu.make_async_copy(held_ref.at[span(row, 1)], ref, sem.at[3 + i])
-        for i, (ref, row) in enumerate(
-            ((near_ref, pick(even, gw - 1, 0)), (far_ref, pick(even, 0, gw - 1)))
-        )
-    ]
-    for copy in rows:
-        copy.start()
+    near_ref[...] = held_ref[span(pick(even, gw - 1, 0), 1)]
+    far_ref[...] = held_ref[span(pick(even, 0, gw - 1), 1)]
     loads[2].wait()
+    loads[3].wait()
     for k, ref in zip(early, outs):
-        listed(held_ref, list_ref, t ^ k, ref)
-    for copy in rows:
-        copy.wait()
-
-
-def second_kernel(dims, late, merged, list_ref, x_ref, near_ref, far_ref, *refs):
+        listed(held_ref, gw * gt, picks_ref, t ^ k, ref)
+
+
+def second_kernel(dims, late, merged, list_ref, held_ref, near_ref, far_ref, *outs):
     gw, gt, cap = dims
-    outs, (held_ref, sem, corner_sem) = refs[:-3], refs[-3:]
     w, t = lax.axis_index("weld"), lax.axis_index("trans")
-    load = load_tiles(x_ref, held_ref, sem)
-    load.start()
-    blank(held_ref)
-    corners, columns = [], []
     even_w, even_t = lax.rem(w, 2) == 0, lax.rem(t, 2) == 0
     for which in range(2):
         if merged:
@@ -113,23 +99,12 @@
         else:
             ref, base = outs[len(late) + which], 0
         column = pick(even_t, gt - 1, 0) if which == 0 else pick(even_t, 0, gt - 1)
-        for i, (corner, place) in enumerate(
-            ((near_ref, pick(even_w, gw + 1, 0)), (far_ref, pick(even_w, 0, gw + 1)))
-        ):
-            copy = pltpu.make_async_copy(
-                corner.at[column], ref.at[base + place], corner_sem.at[2 * which + i]
-            )
-            copy.start()
-            corners.append(copy)
-        columns.append((ref, base, column))
-    load.wait()
-    for ref, base, column in columns:
+        ref[base + pick(even_w, gw + 1, 0)] = near_ref[column]
+        ref[base + pick(even_w, 0, gw + 1)] = far_ref[column]
         for r in range(gw):
             ref[base + 1 + r] = held_ref[r * gt + column]
     for k, ref in zip(late, outs):
-        listed(held_ref, list_ref, t ^ k, ref)
-    for copy in corners:
-        copy.wait()
+        listed(held_ref, gw * gt, list_ref, t ^ k, ref)
 
 
 def tree(terms):
@@ -293,9 +268,14 @@
         functools.partial(first_kernel, (gw, gt), early),
         name="edge_rows",
         out_shape=(stack(gt), stack(gt)) + (stack(cap),) * len(early),
-        in_specs=[SMEM, HBM],
-        out_specs=(HBM, HBM) + (VMEM,) * len(early),
-        scratch_shapes=[buffer(total + 1), pltpu.SemaphoreType.DMA((5,))],
+        in_specs=[HBM, HBM],
+        out_specs=(VMEM,) * (2 + len(early)),
+        scratch_shapes=[
+            pltpu.SMEM((peers, cap), i32),
+            buffer(total),
+            pltpu.SemaphoreType.DMA((6,)),
+        ],
+        compiler_params=pltpu.CompilerParams(vmem_limit_bytes=56 * MIB),
         cost_estimate=cost(0, 2),
     )(lists, tiles)
     near = lax.ppermute(near_out, "weld", pairing(weld, 0))
@@ -328,13 +308,8 @@
         functools.partial(second_kernel, (gw, gt, cap), late, merged),
         name="edge_columns",
         out_shape=tuple(stack(n) for n in lengths),
-        in_specs=[SMEM, HBM, HBM, HBM],
+        in_specs=[SMEM, VMEM, VMEM, VMEM],
         out_specs=(VMEM,) * len(lengths),
-        scratch_shapes=[
-            buffer(total + 1),
-            pltpu.SemaphoreType.DMA,
-            pltpu.SemaphoreType.DMA((4,)),
-        ],
         compiler_params=pltpu.CompilerParams(vmem_limit_bytes=8 * MIB),
         cost_estimate=cost(0, 2),
     )(lists, tiles, near, far)

time: 32.2 us -> 30.2 us (0.938)
  Pallas kernels: 19.7 us -> 17.8 us
    pallas_call x1, Pallas kernels: 9.91 us -> 8.88 us  [on_device(): pl.pallas_call(functools.partial(local_kernel, (gw, gt, entries, UNROLLED...]
    pallas_call x1, Pallas kernels: 3.18 us -> 2.23 us  [on_device(): pl.pallas_call(functools.partial(first_kernel, (gw, gt), early), name='ed...]
where the time goes in v2:
time: 30.2 us; the launch traced here: 30 us
  Pallas kernels  17.8 us (59%)
  starting transfers between devices  11.4 us (38%)
  between operations  0.74 us (2%)
    pallas_call x1, Pallas kernels, on_device(): pl.pallas_call(functools.partial(local_kernel, (gw, gt, entries, UNROLLED...  8.88 us
    ppermute x3, starting transfers between devices, on_device(): got[k] = lax.ppermute(message, 'trans', [(i, i ^ k) for i in range(peers)])  6.84 us
    ppermute x1, starting transfers between devices, on_device(): far = lax.ppermute(far_out, 'weld', pairing(weld, 1))  4.46 us
    pallas_call x1, Pallas kernels, on_device(): pl.pallas_call(functools.partial(finish_kernel, (gw, gt, entries, peers,...  4.27 us
    pallas_call x1, Pallas kernels, on_device(): pl.pallas_call(functools.partial(first_kernel, (gw, gt), early), name='ed...  2.23 us
    pallas_call x1, Pallas kernels, on_device(): pl.pallas_call(functools.partial(index_kernel, (gw, gt, bank, wall_bank,...  1.54 us
    pallas_call x1, Pallas kernels, on_device(): pl.pallas_call(functools.partial(second_kernel, (gw, gt, cap), late, merg...  0.84 us
  transfers between devices with their start and end apart: 5, of which 0 were waited for; matrix products, arithmetic and copies ran while one was open for 0% of the time, Pallas kernels for 38%

profile of v2, /device:TPU:1, one launch (start us, length us, event | category | flops | bytes accessed | tf_op | source)
XLA Modules:
  0.0 30.0 jit_solution(14680120643917989219)
XLA Ops:
  0.6 0.0 copy-start
  0.6 2.2 %edge_rows.1 = (bf16[32,16,128]{2,1,0:T(8,128)(2,1)}, bf16[32,16,128]{2,1,0:T(8,128)(2,1)}, bf16[32,16,128]{2,1,0:T(8,128)(2,1)}) custom-call(s32[4,32]{1,0:T(4,128)} %bitcast.14, bf16[256,16,128]{2,1,0:T(8,128)(2,1)} %bitcast.10), custom_call_target="tpu_custom_call" | custom-call | bytes 2097152 | tf_op jit(solution)/shard_map/edge_rows/pallas_call | solution.py:267
  2.9 0.1 collective-permute-start
  3.0 4.5 %collective-permute-start.1 = (bf16[32,16,128]{2,1,0:T(8,128)(2,1)}, bf16[32,16,128]{2,1,0:T(8,128)(2,1)S(1)}, u32[]{:S(2)}, u32[]{:S(2)}) collective-permute-start(bf16[32,16,128]{2,1,0:T(8,128)(2,1)} %get-tuple-element.14), channel_id=1, source_target_pairs={{4,8},{8,4},{12,16},{16,12},{20,24},{24,20},{5,9},{9,5},{13,17},{1... | collective-permute-start | bytes 393224 | tf_op jit(solution)/shard_map/ppermute | solution.py:282
  7.5 2.4 %collective-permute-start.3 = (bf16[32,16,128]{2,1,0:T(8,128)(2,1)}, bf16[32,16,128]{2,1,0:T(8,128)(2,1)S(1)}, u32[]{:S(2)}, u32[]{:S(2)}) collective-permute-start(bf16[32,16,128]{2,1,0:T(8,128)(2,1)} %get-tuple-element.17), channel_id=1, source_target_pairs={{0,2},{1,3},{2,0},{3,1},{4,6},{5,7},{6,4},{7,5},{8,10},{9,11},{10,... | collective-permute-start | bytes 393224 | tf_op jit(solution)/shard_map/ppermute | solution.py:285
  9.8 0.0 copy-start.4
  9.8 1.5 %pair_index.1 = (s32[12,8,128]{2,1,0:T(8,128)}, s32[12,8,128]{2,1,0:T(8,128)}) custom-call(s32[12,8,32]{2,1,0:T(8,128)} %bitcast.18, s32[12,8,32]{2,1,0:T(8,128)} %bitcast.19, s32[16,16]{1,0:T(8,128)} %bitcast.20, s32[16,16]{1,0:T(8,128)} %bitcast.21), custom_call_target="tpu_custom_call" | custom-call | flops 1000000 | bytes 3145728 | tf_op jit(solution)/shard_map/pair_index/pallas_call | solution.py:288
  11.4 0.0 copy-start.1
  11.4 0.0 copy-start.5
  11.4 0.0 collective-permute-done.near_ref
  11.4 0.0 collective-permute-done.1.far_ref
  11.4 0.0 copy-done
  11.4 0.0 copy-done.4
  11.4 0.8 %edge_columns.1 = (bf16[42,16,128]{2,1,0:T(8,128)(2,1)S(1)}, bf16[42,16,128]{2,1,0:T(8,128)(2,1)S(1)}, bf16[32,16,128]{2,1,0:T(8,128)(2,1)S(1)}) custom-call(s32[4,32]{1,0:T(4,128)S(1)} %bitcast.15, bf16[256,16,128]{2,1,0:T(8,128)(2,1)S(1)} %bitcast.11, bf16[32,16,128]{2,1,0:T(8,128)(2,1)S(1)} %collective-permute-done.near_ref, ...), custom_call_target="tpu_custom_call" | custom-call | bytes 2097152 | tf_op jit(solution)/shard_map/edge_columns/pallas_call | solution.py:307
  12.3 2.0 %collective-permute-start.2 = (bf16[42,16,128]{2,1,0:T(8,128)(2,1)S(1)}, bf16[42,16,128]{2,1,0:T(8,128)(2,1)S(1)}, u32[]{:S(2)}, u32[]{:S(2)}) collective-permute-start(bf16[42,16,128]{2,1,0:T(8,128)(2,1)S(1)} %get-tuple-element.16), channel_id=1, source_target_pairs={{0,1},{1,0},{2,3},{3,2},{4,5},{5,4},{6,7},{7,6},{8,9},{9,8},{10,11... | collective-permute-start | bytes 516104 | tf_op jit(solution)/shard_map/ppermute | solution.py:318
  14.3 2.5 %collective-permute-start.4 = (bf16[42,16,128]{2,1,0:T(8,128)(2,1)S(1)}, bf16[42,16,128]{2,1,0:T(8,128)(2,1)S(1)}, u32[]{:S(2)}, u32[]{:S(2)}) collective-permute-start(bf16[42,16,128]{2,1,0:T(8,128)(2,1)S(1)} %get-tuple-element.18), channel_id=1, source_target_pairs={{0,3},{1,2},{2,1},{3,0},{4,7},{5,6},{6,5},{7,4},{8,11},{9,10},{10,... | collective-permute-start | bytes 516104 | tf_op jit(solution)/shard_map/ppermute | solution.py:318
  16.7 0.0 copy-done.1
  16.7 0.0 copy-done.5
  16.7 0.0 copy-start.2
  16.8 0.0 copy-start.3
  16.8 8.9 %local_pairs.1 = bf16[256,16,128]{2,1,0:T(8,128)(2,1)} custom-call(s32[96,128]{1,0:T(8,128)S(1)} %bitcast.16, bf16[256,16,128]{2,1,0:T(8,128)(2,1)S(1)} %bitcast.12, bf16[32,16,128]{2,1,0:T(8,128)(2,1)S(1)} %collective-permute-done.near_ref, bf16[32,16,128]{2,1,0:T(8,128)(2,1)S(1)} %collective-permute-done.1.far_ref, bf16[16,128,128]{2,1,0:T(8,128)(2,1)S(1)} %copy-done.1), custom_call_target="tpu_custom_call" | custom-call | flops 2684354560 | bytes 31457280 | tf_op jit(solution)/shard_map/local_pairs/pallas_call | solution.py:327
  25.6 0.0 collective-permute-done.3.refs_2_
  25.7 0.0 collective-permute-done.2.refs_1_
  25.7 0.0 collective-permute-done.4.refs_3_
  25.7 0.0 copy-done.2
  25.7 0.0 copy-done.3
  25.7 4.3 %columns_and_walls.1 = (bf16[8,32,16,128]{3,2,1,0:T(8,128)(2,1)}, bf16[16,16,128]{2,1,0:T(8,128)(2,1)}) custom-call(s32[96,128]{1,0:T(8,128)S(1)} %bitcast.13, bf16[32,16,128]{2,1,0:T(8,128)(2,1)S(1)} %get-tuple-element.15.refs_0_, bf16[42,16,128]{2,1,0:T(8,128)(2,1)S(1)} %collective-permute-done.2.refs_1_, ...), custom_call_target="tpu_custom_call", output_to_operand_aliasing={{0}: (7, {})} | custom-call | flops 536870912 | bytes 8388608 | tf_op jit(solution)/shard_map/columns_and_walls/pallas_call | solution.py:346
Async XLA Ops:
  0.6 10.8 %copy-start = (bf16[8,32,16,128]{3,2,1,0:T(8,128)(2,1)S(1)}, bf16[8,32,16,128]{3,2,1,0:T(8,128)(2,1)}, u32[]{:S(2)}) copy-start(bf16[8,32,16,128]{3,2,1,0:T(8,128)(2,1)} %param.8) | copy-start | bytes 3145732
  2.9 8.5 %collective-permute-start = (bf16[32,16,128]{2,1,0:T(8,128)(2,1)}, bf16[32,16,128]{2,1,0:T(8,128)(2,1)S(1)}, u32[]{:S(2)}, u32[]{:S(2)}) collective-permute-start(bf16[32,16,128]{2,1,0:T(8,128)(2,1)} %get-tuple-element.13), channel_id=1, source_target_pairs={{0,4},{4,0},{8,12},{12,8},{16,20},{20,16},{24,28},{28,24},{1,5},{5... | collective-permute-start | bytes 393224 | tf_op jit(solution)/shard_map/ppermute | solution.py:281
  3.0 8.4 %collective-permute-start.1 = (bf16[32,16,128]{2,1,0:T(8,128)(2,1)}, bf16[32,16,128]{2,1,0:T(8,128)(2,1)S(1)}, u32[]{:S(2)}, u32[]{:S(2)}) collective-permute-start(bf16[32,16,128]{2,1,0:T(8,128)(2,1)} %get-tuple-element.14), channel_id=1, source_target_pairs={{4,8},{8,4},{12,16},{16,12},{20,24},{24,20},{5,9},{9,5},{13,17},{1... | collective-permute-start | bytes 393224 | tf_op jit(solution)/shard_map/ppermute | solution.py:282
  7.5 18.2 %collective-permute-start.3 = (bf16[32,16,128]{2,1,0:T(8,128)(2,1)}, bf16[32,16,128]{2,1,0:T(8,128)(2,1)S(1)}, u32[]{:S(2)}, u32[]{:S(2)}) collective-permute-start(bf16[32,16,128]{2,1,0:T(8,128)(2,1)} %get-tuple-element.17), channel_id=1, source_target_pairs={{0,2},{1,3},{2,0},{3,1},{4,6},{5,7},{6,4},{7,5},{8,10},{9,11},{10,... | collective-permute-start | bytes 393224 | tf_op jit(solution)/shard_map/ppermute | solution.py:285
  9.8 1.6 %copy-start.4 = (s32[1,1,4,32]{3,2,1,0:T(4,128)S(1)}, s32[1,1,4,32]{3,2,1,0:T(4,128)}, u32[]{:S(2)}) copy-start(s32[1,1,4,32]{3,2,1,0:T(4,128)} %param.12) | copy-start | bytes 1540
  11.4 5.4 %copy-start.1 = (bf16[16,128,128]{2,1,0:T(8,128)(2,1)S(1)}, bf16[16,128,128]{2,1,0:T(8,128)(2,1)}, u32[]{:S(2)}) copy-start(bf16[16,128,128]{2,1,0:T(8,128)(2,1)} %refs_4_.1) | copy-start | bytes 1572868
  11.4 5.4 %copy-start.5 = (s32[12,8,128]{2,1,0:T(8,128)S(1)}, s32[12,8,128]{2,1,0:T(8,128)}, u32[]{:S(2)}) copy-start(s32[12,8,128]{2,1,0:T(8,128)} %get-tuple-element.19) | copy-start | bytes 147460
  12.3 13.4 %collective-permute-start.2 = (bf16[42,16,128]{2,1,0:T(8,128)(2,1)S(1)}, bf16[42,16,128]{2,1,0:T(8,128)(2,1)S(1)}, u32[]{:S(2)}, u32[]{:S(2)}) collective-permute-start(bf16[42,16,128]{2,1,0:T(8,128)(2,1)S(1)} %get-tuple-element.16), channel_id=1, source_target_pairs={{0,1},{1,0},{2,3},{3,2},{4,5},{5,4},{6,7},{7,6},{8,9},{9,8},{10,11... | collective-permute-start | bytes 516104 | tf_op jit(solution)/shard_map/ppermute | solution.py:318
  14.3 11.4 %collective-permute-start.4 = (bf16[42,16,128]{2,1,0:T(8,128)(2,1)S(1)}, bf16[42,16,128]{2,1,0:T(8,128)(2,1)S(1)}, u32[]{:S(2)}, u32[]{:S(2)}) collective-permute-start(bf16[42,16,128]{2,1,0:T(8,128)(2,1)S(1)} %get-tuple-element.18), channel_id=1, source_target_pairs={{0,3},{1,2},{2,1},{3,0},{4,7},{5,6},{6,5},{7,4},{8,11},{9,10},{10,... | collective-permute-start | bytes 516104 | tf_op jit(solution)/shard_map/ppermute | solution.py:318
  16.7 8.9 %copy-start.2 = (bf16[8,128,128]{2,1,0:T(8,128)(2,1)S(1)}, bf16[8,128,128]{2,1,0:T(8,128)(2,1)}, u32[]{:S(2)}) copy-start(bf16[8,128,128]{2,1,0:T(8,128)(2,1)} %refs_5_.1) | copy-start | bytes 786436
  16.8 8.9 %copy-start.3 = (s32[12,8,128]{2,1,0:T(8,128)S(1)}, s32[12,8,128]{2,1,0:T(8,128)}, u32[]{:S(2)}) copy-start(s32[12,8,128]{2,1,0:T(8,128)} %get-tuple-element.12) | copy-start | bytes 147460

commit v3 on v2

--- a/solution.py
+++ b/solution.py
@@ -12,14 +12,15 @@
 HBM = pl.BlockSpec(memory_space=pl.ANY)
 MIB = 1 << 20
 UNROLLED = True
-WALL_LANE = 64
+LANES = 128
+WALL_LANE = 32
 
 
 def pick(cond, a, b):
     return lax.select(cond, jnp.int32(a), jnp.int32(b))
 
 
-def index_kernel(dims, off_ref, kind_ref, slot_ref, wkind_ref, local_ref, side_ref):
+def index_kernel(dims, off_ref, kind_ref, slot_ref, wkind_ref, out_ref):
     gw, gt, bank, wall_bank, peers, cap = dims
     t = lax.axis_index("trans")
     off, kind = off_ref[...], kind_ref[...]
@@ -30,16 +31,19 @@
     left, right = col < 0, col >= gt
     side = left | right
     rows = gw // 2 + 2
-    local_ref[:, :, :gt] = jnp.where(
-        side, bank * rows * gt, kind * (rows * gt) + band * gt + col
-    )
+    local = jnp.where(side, bank * rows * gt, kind * (rows * gt) + band * gt + col)
+    pack = LANES // gt
+    for n in range(off.shape[0]):
+        out_ref[n // pack, :, n % pack * gt : (n % pack + 1) * gt] = local[n]
     even_t = lax.rem(t, 2) == 0
     depth = gw + 2
     base = jnp.where(left, pick(even_t, depth, 0), pick(even_t, 0, depth))
     edge = (left & (t == 0)) | (right & (t == peers - 1))
-    side_ref[:, :, :gt] = jnp.where(
-        side & ~edge, kind * (2 * depth) + base + row + dr, bank * 2 * depth
-    )
+    sides = jnp.where(side & ~edge, kind * (2 * depth) + base + row + dr, bank * 2 * depth)
+    last = out_ref.shape[0] - 1
+    for n in range(off.shape[0]):
+        out_ref[last, :, 2 * n : 2 * n + 1] = sides[n, :, :1]
+        out_ref[last, :, 2 * n + 1 : 2 * n + 2] = sides[n, :, gt - 1 :]
     slot = slot_ref[...]
     sender = slot // cap
     wall = jnp.where(
@@ -47,8 +51,10 @@
         wall_bank * peers * cap,
         wkind_ref[...] * (peers * cap) + (sender ^ t) * cap + (slot - sender * cap),
     )
+    picks = slot.shape[1]
     for q in range(slot.shape[0] // gw):
-        side_ref[q, :, WALL_LANE : WALL_LANE + slot.shape[1]] = wall[q * gw : (q + 1) * gw]
+        at = WALL_LANE + q * picks
+        out_ref[last, :, at : at + picks] = wall[q * gw : (q + 1) * gw]
 
 
 def blank(ref):
@@ -126,11 +132,12 @@
 
 def local_kernel(dims, index_ref, x_ref, near_ref, far_ref, bank, out_ref, *scratch):
     gw, gt, entries, unrolled = dims
-    index, top, low, total, index_sem, sem = scratch
+    index, top, low, sem = scratch
+    pack = LANES // gt
     even = lax.rem(lax.axis_index("weld"), 2) == 0
     half, kernels = gw // 2, bank.shape[0]
     step = (half + 2) * gt
-    fetch = pltpu.make_async_copy(index_ref, index, index_sem)
+    fetch = pltpu.make_async_copy(index_ref.at[: entries // pack], index, sem)
     fetch.start()
     blank(top)
     blank(low)
@@ -138,8 +145,11 @@
     after = jnp.where(even, near_ref[...], far_ref[...])
 
     def gather(table, r, c):
-        terms = [table[index[n * gw + r, c]].astype(jnp.float32) for n in range(entries)]
-        total[r * gt + c] = tree(terms).astype(total.dtype)
+        terms = [
+            table[index[n // pack, r, n % pack * gt + c]].astype(jnp.float32)
+            for n in range(entries)
+        ]
+        out_ref[r * gt + c] = tree(terms).astype(out_ref.dtype)
 
     upper = [(top, step, 0, 0, step), (low, step, 0, half * gt, 2 * gt)]
     lower = [(low, step, 2 * gt, 0, half * gt)]
@@ -157,44 +167,43 @@
             for r, c in cells[j // 2 * share : (j // 2 + 1) * share]:
                 gather(top, r, c)
 
-    def store(first, count, i):
-        span = pl.ds(first * gt, count * gt)
-        copy = pltpu.make_async_copy(total.at[span], out_ref.at[span], sem.at[i])
-        copy.start()
-        return copy
-
     def body(r, _, table):
         for c in range(gt):
             gather(table, r, c)
         return 0
 
-    if not unrolled:
+    if unrolled:
+        for r in range(half, gw):
+            body(r, 0, low)
+    else:
         lax.fori_loop(0, half, functools.partial(body, table=top), 0)
-    stores = [store(0, half, 0)]
-    for i, first in enumerate(range(half, gw, half // 2)):
-        if unrolled:
-            for r in range(first, first + half // 2):
-                body(r, 0, low)
-        else:
-            lax.fori_loop(first, first + half // 2, functools.partial(body, table=low), 0)
-        stores.append(store(first, half // 2, 1 + i))
-    for copy in stores:
-        copy.wait()
-
-
-def finish_kernel(dims, side_hbm, *refs):
+        lax.fori_loop(half, gw, functools.partial(body, table=low), 0)
+
+
+def finish_kernel(dims, index_ref, *refs):
     gw, gt, entries, peers, cap, walls, picks, merged = dims
     own_ref = refs[0]
     count = peers - 1 + (0 if merged else 2)
     got = refs[1 : 1 + count]
-    bank_ref, wall_bank_ref, _, rates_ref, walls_ref = refs[1 + count : 6 + count]
-    side_ref, table_ref, wall_table_ref, cols_ref, in_sem, out_sem = refs[6 + count :]
-    edges = [(rates_ref.at[:, c], cols_ref.at[e]) for e, c in enumerate((0, gt - 1))]
-    fetch = [pltpu.make_async_copy(a, b, in_sem.at[e]) for e, (a, b) in enumerate(edges)]
-    store = [pltpu.make_async_copy(b, a, out_sem.at[e]) for e, (a, b) in enumerate(edges)]
-    fetch.append(pltpu.make_async_copy(side_hbm, side_ref, in_sem.at[2]))
-    for copy in fetch:
-        copy.start()
+    bank_ref, wall_bank_ref, local_ref, rates_ref, walls_ref = refs[1 + count : 6 + count]
+    index, table_ref, wall_table_ref, cols_ref, done_ref, sem = refs[6 + count :]
+    fetch = pltpu.make_async_copy(index_ref.at[index_ref.shape[0] - 1], index, sem.at[0])
+    inner = pltpu.make_async_copy(
+        local_ref.at[:, 1 : gt - 1], rates_ref.at[:, 1 : gt - 1], sem.at[1]
+    )
+    edges = [
+        pltpu.make_async_copy(cols_ref.at[e], rates_ref.at[:, c], sem.at[2 + e])
+        for e, c in enumerate((0, gt - 1))
+    ]
+    part = walls // 2
+    ready = [
+        pltpu.make_async_copy(
+            done_ref.at[pl.ds(h * part, part)], walls_ref.at[pl.ds(h * part, part)], sem.at[4 + h]
+        )
+        for h in range(2)
+    ]
+    fetch.start()
+    inner.start()
     depth = gw + 2
     if merged:
         sides = [got[0][cap : cap + depth], got[2][cap : cap + depth]]
@@ -210,23 +219,23 @@
     received = received.reshape(slots * 16, 128)
     for j in range(0, wall_bank_ref.shape[0], 2):
         products(received, wall_bank_ref, j, [(wall_table_ref, slots, 0, 0, slots)])
-    for copy in fetch:
-        copy.wait()
+    fetch.wait()
     for e, c in enumerate((0, gt - 1)):
         for r in range(gw):
-            terms = [
-                table_ref[side_ref[n * gw + r, c]].astype(jnp.float32) for n in range(entries)
-            ]
-            base = cols_ref[e, r].astype(jnp.float32)
+            terms = [table_ref[index[r, 2 * n + e]].astype(jnp.float32) for n in range(entries)]
+            base = local_ref[r, c].astype(jnp.float32)
             cols_ref[e, r] = (base + tree(terms)).astype(cols_ref.dtype)
-        store[e].start()
+        edges[e].start()
     for j in range(walls):
+        lane = WALL_LANE + j // gw * picks
         picked = [
-            wall_table_ref[side_ref[j, WALL_LANE + m]].astype(jnp.float32) for m in range(picks)
+            wall_table_ref[index[j % gw, lane + m]].astype(jnp.float32) for m in range(picks)
         ]
         sums = tree(picked)
-        walls_ref[j] = (sums / (1.0 + sums[0:1, :])).astype(walls_ref.dtype)
-    for copy in store:
+        done_ref[j] = (sums / (1.0 + sums[0:1, :])).astype(done_ref.dtype)
+        if (j + 1) % part == 0:
+            ready[j // part].start()
+    for copy in (inner, *edges, *ready):
         copy.wait()
 
 
@@ -284,13 +293,13 @@
     for k, message in zip(early, early_out):
         got[k] = lax.ppermute(message, "trans", [(i, i ^ k) for i in range(peers)])
 
-    table_index = jax.ShapeDtypeStruct((entries, gw, 128), i32)
-    local_index, side_index = pl.pallas_call(
+    planes = entries * gt // LANES + 1
+    index = pl.pallas_call(
         functools.partial(index_kernel, (gw, gt, bank, wall_bank, peers, cap)),
         name="pair_index",
-        out_shape=(table_index, table_index),
+        out_shape=jax.ShapeDtypeStruct((planes, gw, LANES), i32),
         in_specs=[VMEM] * 4,
-        out_specs=(VMEM, VMEM),
+        out_specs=VMEM,
         cost_estimate=cost(1_000_000, 3),
     )(
         pair_offsets.transpose(2, 0, 1),
@@ -298,8 +307,6 @@
         wall_slots.reshape(walls, picks),
         wall_kernel.reshape(walls, picks),
     )
-    local_index = local_index.reshape(entries * gw, 128)
-    side_index = side_index.reshape(entries * gw, 128)
 
     lengths = [cap + (depth if merged and k else 0) for k in late]
     if not merged:
@@ -329,39 +336,36 @@
         name="local_pairs",
         out_shape=stack(total),
         in_specs=[HBM] + [VMEM] * 4,
-        out_specs=HBM,
+        out_specs=VMEM,
         scratch_shapes=[
-            pltpu.SMEM((entries * gw, 128), i32),
+            pltpu.SMEM((planes - 1, gw, LANES), i32),
             buffer(bank * step + 1),
             buffer(bank * step + 1),
-            buffer(total),
             pltpu.SemaphoreType.DMA,
-            pltpu.SemaphoreType.DMA((3,)),
         ],
         compiler_params=pltpu.CompilerParams(vmem_limit_bytes=44 * MIB),
         cost_estimate=cost(2 * (gw + 2) * gt * channels * tile * tile * bank, 30),
-    )(local_index, tiles, near, far, kernels)
+    )(index, tiles, near, far, kernels)
 
     count = len(received)
     rates, wall_out = pl.pallas_call(
         functools.partial(finish_kernel, (gw, gt, entries, peers, cap, walls, picks, merged)),
         name="columns_and_walls",
         out_shape=(jax.ShapeDtypeStruct((gw, gt, channels, tile), bf16), stack(walls)),
-        in_specs=[HBM] + [VMEM] * (3 + count) + [HBM],
-        out_specs=(HBM, VMEM),
+        in_specs=[HBM] + [VMEM] * (4 + count),
+        out_specs=(HBM, HBM),
         scratch_shapes=[
-            pltpu.SMEM((entries * gw, 128), i32),
+            pltpu.SMEM((gw, LANES), i32),
             buffer(bank * 2 * depth + 1),
             buffer(wall_bank * peers * cap + 1),
             pltpu.VMEM((2, gw, channels, tile), bf16),
-            pltpu.SemaphoreType.DMA((3,)),
-            pltpu.SemaphoreType.DMA((2,)),
+            buffer(walls),
+            pltpu.SemaphoreType.DMA((6,)),
         ],
-        input_output_aliases={4 + count: 0},
         compiler_params=pltpu.CompilerParams(vmem_limit_bytes=44 * MIB),
         cost_estimate=cost(2 * peers * cap * channels * tile * tile * wall_bank, 8),
     )(
-        side_index,
+        index,
         own,
         *received,
         kernels,

time: 30.2 us -> 26.9 us (0.89)
  Pallas kernels: 17.8 us -> 14.5 us
    pallas_call x1, Pallas kernels: 8.88 us -> 7.24 us  [on_device(): pl.pallas_call(functools.partial(local_kernel, (gw, gt, entries, UNROLLED...]
    pallas_call x1, Pallas kernels: 4.27 us -> 2.64 us  [on_device(): pl.pallas_call(functools.partial(finish_kernel, (gw, gt, entries, peers,...]
  transfers between devices with their start and end apart: 5 -> 5, of which waited for: 0 -> 0; matrix products, arithmetic and copies ran while one was open for 0% -> 0% of each run, Pallas kernels for 38% -> 36%
where the time goes in v3:
time: 26.9 us; the launch traced here: 26.7 us
  Pallas kernels  14.5 us (54%)
  starting transfers between devices  11.4 us (42%)
  between operations  0.73 us (3%)
    pallas_call x1, Pallas kernels, on_device(): pl.pallas_call(functools.partial(local_kernel, (gw, gt, entries, UNROLLED...  7.24 us
    ppermute x3, starting transfers between devices, on_device(): got[k] = lax.ppermute(message, 'trans', [(i, i ^ k) for i in range(peers)])  6.81 us
    ppermute x1, starting transfers between devices, on_device(): far = lax.ppermute(far_out, 'weld', pairing(weld, 1))  4.46 us
    pallas_call x1, Pallas kernels, on_device(): pl.pallas_call(functools.partial(finish_kernel, (gw, gt, entries, peers,...  2.64 us
    pallas_call x1, Pallas kernels, on_device(): pl.pallas_call(functools.partial(first_kernel, (gw, gt), early), name='ed...  2.23 us
    pallas_call x1, Pallas kernels, on_device(): pl.pallas_call(functools.partial(index_kernel, (gw, gt, bank, wall_bank,...  1.57 us
    pallas_call x1, Pallas kernels, on_device(): pl.pallas_call(functools.partial(second_kernel, (gw, gt, cap), late, merg...  0.84 us
  transfers between devices with their start and end apart: 5, of which 0 were waited for; matrix products, arithmetic and copies ran while one was open for 0% of the time, Pallas kernels for 36%

profile of v3, /device:TPU:1, one launch (start us, length us, event | category | flops | bytes accessed | tf_op | source)
XLA Modules:
  0.0 26.7 jit_solution(15727901872106881967)
XLA Ops:
  0.6 0.0 copy-start
  0.6 2.2 %edge_rows.1 = (bf16[32,16,128]{2,1,0:T(8,128)(2,1)}, bf16[32,16,128]{2,1,0:T(8,128)(2,1)}, bf16[32,16,128]{2,1,0:T(8,128)(2,1)}) custom-call(s32[4,32]{1,0:T(4,128)} %bitcast.12, bf16[256,16,128]{2,1,0:T(8,128)(2,1)} %bitcast.8), custom_call_target="tpu_custom_call" | custom-call | bytes 2097152 | tf_op jit(solution)/shard_map/edge_rows/pallas_call | solution.py:276
  2.9 0.1 collective-permute-start
  3.0 4.5 %collective-permute-start.1 = (bf16[32,16,128]{2,1,0:T(8,128)(2,1)}, bf16[32,16,128]{2,1,0:T(8,128)(2,1)S(1)}, u32[]{:S(2)}, u32[]{:S(2)}) collective-permute-start(bf16[32,16,128]{2,1,0:T(8,128)(2,1)} %get-tuple-element.11), channel_id=1, source_target_pairs={{4,8},{8,4},{12,16},{16,12},{20,24},{24,20},{5,9},{9,5},{13,17},{1... | collective-permute-start | bytes 393224 | tf_op jit(solution)/shard_map/ppermute | solution.py:291
  7.5 2.4 %collective-permute-start.3 = (bf16[32,16,128]{2,1,0:T(8,128)(2,1)}, bf16[32,16,128]{2,1,0:T(8,128)(2,1)S(1)}, u32[]{:S(2)}, u32[]{:S(2)}) collective-permute-start(bf16[32,16,128]{2,1,0:T(8,128)(2,1)} %get-tuple-element.14), channel_id=1, source_target_pairs={{0,2},{1,3},{2,0},{3,1},{4,6},{5,7},{6,4},{7,5},{8,10},{9,11},{10,... | collective-permute-start | bytes 393224 | tf_op jit(solution)/shard_map/ppermute | solution.py:294
  9.8 0.0 copy-start.4
  9.8 1.6 %pair_index.1.index_ref = s32[4,8,128]{2,1,0:T(8,128)} custom-call(s32[12,8,32]{2,1,0:T(8,128)} %bitcast.14, s32[12,8,32]{2,1,0:T(8,128)} %bitcast.15, s32[16,16]{1,0:T(8,128)} %bitcast.16, s32[16,16]{1,0:T(8,128)} %bitcast.17), custom_call_target="tpu_custom_call" | custom-call | flops 1000000 | bytes 3145728 | tf_op jit(solution)/shard_map/pair_index/pallas_call | solution.py:297
  11.4 0.0 copy-start.1
  11.4 0.0 copy-start.3
  11.4 0.0 collective-permute-done.near_ref
  11.4 0.0 collective-permute-done.1.far_ref
  11.4 0.0 copy-done
  11.4 0.0 copy-done.4
  11.5 0.8 %edge_columns.1 = (bf16[42,16,128]{2,1,0:T(8,128)(2,1)S(1)}, bf16[42,16,128]{2,1,0:T(8,128)(2,1)S(1)}, bf16[32,16,128]{2,1,0:T(8,128)(2,1)S(1)}) custom-call(s32[4,32]{1,0:T(4,128)S(1)} %bitcast.13, bf16[256,16,128]{2,1,0:T(8,128)(2,1)S(1)} %bitcast.9, bf16[32,16,128]{2,1,0:T(8,128)(2,1)S(1)} %collective-permute-done.near_ref, ...), custom_call_target="tpu_custom_call" | custom-call | bytes 2097152 | tf_op jit(solution)/shard_map/edge_columns/pallas_call | solution.py:314
  12.3 1.9 %collective-permute-start.2 = (bf16[42,16,128]{2,1,0:T(8,128)(2,1)S(1)}, bf16[42,16,128]{2,1,0:T(8,128)(2,1)S(1)}, u32[]{:S(2)}, u32[]{:S(2)}) collective-permute-start(bf16[42,16,128]{2,1,0:T(8,128)(2,1)S(1)} %get-tuple-element.13), channel_id=1, source_target_pairs={{0,1},{1,0},{2,3},{3,2},{4,5},{5,4},{6,7},{7,6},{8,9},{9,8},{10,11... | collective-permute-start | bytes 516104 | tf_op jit(solution)/shard_map/ppermute | solution.py:325
  14.3 0.0 copy-start.2
  14.3 2.5 %collective-permute-start.4 = (bf16[42,16,128]{2,1,0:T(8,128)(2,1)S(1)}, bf16[42,16,128]{2,1,0:T(8,128)(2,1)S(1)}, u32[]{:S(2)}, u32[]{:S(2)}) collective-permute-start(bf16[42,16,128]{2,1,0:T(8,128)(2,1)S(1)} %get-tuple-element.15), channel_id=1, source_target_pairs={{0,3},{1,2},{2,1},{3,0},{4,7},{5,6},{6,5},{7,4},{8,11},{9,10},{10,... | collective-permute-start | bytes 516104 | tf_op jit(solution)/shard_map/ppermute | solution.py:325
  16.7 0.0 copy-done.1
  16.7 0.0 copy-done.3
  16.8 7.2 %local_pairs.1 = bf16[256,16,128]{2,1,0:T(8,128)(2,1)S(1)} custom-call(s32[4,8,128]{2,1,0:T(8,128)S(1)} %copy-done.3, bf16[256,16,128]{2,1,0:T(8,128)(2,1)S(1)} %bitcast.10, bf16[32,16,128]{2,1,0:T(8,128)(2,1)S(1)} %collective-permute-done.near_ref, bf16[32,16,128]{2,1,0:T(8,128)(2,1)S(1)} %collective-permute-done.1.far_ref, bf16[16,128,128]{2,1,0:T(8,128)(2,1)S(1)} %copy-done.1), custom_call_target="tpu_custom_call" | custom-call | flops 2684354560 | bytes 31457280 | tf_op jit(solution)/shard_map/local_pairs/pallas_call | solution.py:334
  24.0 0.0 collective-permute-done.3.refs_2_
  24.0 0.0 collective-permute-done.2.refs_1_
  24.0 0.0 collective-permute-done.4.refs_3_
  24.0 0.0 copy-done.2
  24.0 2.6 %columns_and_walls.1 = (bf16[8,32,16,128]{3,2,1,0:T(8,128)(2,1)}, bf16[16,16,128]{2,1,0:T(8,128)(2,1)}) custom-call(s32[4,8,128]{2,1,0:T(8,128)S(1)} %copy-done.3, bf16[32,16,128]{2,1,0:T(8,128)(2,1)S(1)} %get-tuple-element.12.refs_0_, bf16[42,16,128]{2,1,0:T(8,128)(2,1)S(1)} %collective-permute-done.2.refs_1_, ...), custom_call_target="tpu_custom_call" | custom-call | flops 536870912 | bytes 8388608 | tf_op jit(solution)/shard_map/columns_and_walls/pallas_call | solution.py:351
Async XLA Ops:
  0.6 10.8 %copy-start = (bf16[8,32,16,128]{3,2,1,0:T(8,128)(2,1)S(1)}, bf16[8,32,16,128]{3,2,1,0:T(8,128)(2,1)}, u32[]{:S(2)}) copy-start(bf16[8,32,16,128]{3,2,1,0:T(8,128)(2,1)} %param.8) | copy-start | bytes 3145732
  2.9 8.5 %collective-permute-start = (bf16[32,16,128]{2,1,0:T(8,128)(2,1)}, bf16[32,16,128]{2,1,0:T(8,128)(2,1)S(1)}, u32[]{:S(2)}, u32[]{:S(2)}) collective-permute-start(bf16[32,16,128]{2,1,0:T(8,128)(2,1)} %get-tuple-element.10), channel_id=1, source_target_pairs={{0,4},{4,0},{8,12},{12,8},{16,20},{20,16},{24,28},{28,24},{1,5},{5... | collective-permute-start | bytes 393224 | tf_op jit(solution)/shard_map/ppermute | solution.py:290
  3.0 8.4 %collective-permute-start.1 = (bf16[32,16,128]{2,1,0:T(8,128)(2,1)}, bf16[32,16,128]{2,1,0:T(8,128)(2,1)S(1)}, u32[]{:S(2)}, u32[]{:S(2)}) collective-permute-start(bf16[32,16,128]{2,1,0:T(8,128)(2,1)} %get-tuple-element.11), channel_id=1, source_target_pairs={{4,8},{8,4},{12,16},{16,12},{20,24},{24,20},{5,9},{9,5},{13,17},{1... | collective-permute-start | bytes 393224 | tf_op jit(solution)/shard_map/ppermute | solution.py:291
  7.5 16.5 %collective-permute-start.3 = (bf16[32,16,128]{2,1,0:T(8,128)(2,1)}, bf16[32,16,128]{2,1,0:T(8,128)(2,1)S(1)}, u32[]{:S(2)}, u32[]{:S(2)}) collective-permute-start(bf16[32,16,128]{2,1,0:T(8,128)(2,1)} %get-tuple-element.14), channel_id=1, source_target_pairs={{0,2},{1,3},{2,0},{3,1},{4,6},{5,7},{6,4},{7,5},{8,10},{9,11},{10,... | collective-permute-start | bytes 393224 | tf_op jit(solution)/shard_map/ppermute | solution.py:294
  9.8 1.6 %copy-start.4 = (s32[1,1,4,32]{3,2,1,0:T(4,128)S(1)}, s32[1,1,4,32]{3,2,1,0:T(4,128)}, u32[]{:S(2)}) copy-start(s32[1,1,4,32]{3,2,1,0:T(4,128)} %param.12) | copy-start | bytes 1540
  11.4 5.3 %copy-start.1 = (bf16[16,128,128]{2,1,0:T(8,128)(2,1)S(1)}, bf16[16,128,128]{2,1,0:T(8,128)(2,1)}, u32[]{:S(2)}) copy-start(bf16[16,128,128]{2,1,0:T(8,128)(2,1)} %refs_4_.1) | copy-start | bytes 1572868
  11.4 5.3 %copy-start.3 = (s32[4,8,128]{2,1,0:T(8,128)S(1)}, s32[4,8,128]{2,1,0:T(8,128)}, u32[]{:S(2)}) copy-start(s32[4,8,128]{2,1,0:T(8,128)} %pair_index.1.index_ref) | copy-start | bytes 49156
  12.3 11.7 %collective-permute-start.2 = (bf16[42,16,128]{2,1,0:T(8,128)(2,1)S(1)}, bf16[42,16,128]{2,1,0:T(8,128)(2,1)S(1)}, u32[]{:S(2)}, u32[]{:S(2)}) collective-permute-start(bf16[42,16,128]{2,1,0:T(8,128)(2,1)S(1)} %get-tuple-element.13), channel_id=1, source_target_pairs={{0,1},{1,0},{2,3},{3,2},{4,5},{5,4},{6,7},{7,6},{8,9},{9,8},{10,11... | collective-permute-start | bytes 516104 | tf_op jit(solution)/shard_map/ppermute | solution.py:325
  14.3 9.8 %copy-start.2 = (bf16[8,128,128]{2,1,0:T(8,128)(2,1)S(1)}, bf16[8,128,128]{2,1,0:T(8,128)(2,1)}, u32[]{:S(2)}) copy-start(bf16[8,128,128]{2,1,0:T(8,128)(2,1)} %refs_5_.1) | copy-start | bytes 786436
  14.3 9.8 %collective-permute-start.4 = (bf16[42,16,128]{2,1,0:T(8,128)(2,1)S(1)}, bf16[42,16,128]{2,1,0:T(8,128)(2,1)S(1)}, u32[]{:S(2)}, u32[]{:S(2)}) collective-permute-start(bf16[42,16,128]{2,1,0:T(8,128)(2,1)S(1)} %get-tuple-element.15), channel_id=1, source_target_pairs={{0,3},{1,2},{2,1},{3,0},{4,7},{5,6},{6,5},{7,4},{8,11},{9,10},{10,... | collective-permute-start | bytes 516104 | tf_op jit(solution)/shard_map/ppermute | solution.py:325

commit v4 on v3

--- a/solution.py
+++ b/solution.py
@@ -11,7 +11,7 @@
 VMEM = pl.BlockSpec(memory_space=pltpu.VMEM)
 HBM = pl.BlockSpec(memory_space=pl.ANY)
 MIB = 1 << 20
-UNROLLED = True
+GROUPS = 2
 LANES = 128
 WALL_LANE = 32
 
@@ -26,11 +26,12 @@
     off, kind = off_ref[...], kind_ref[...]
     dr = (off * 11) >> 5
     row = lax.broadcasted_iota(jnp.int32, off.shape, 1)
-    band = row + dr - jnp.where(row < gw // 2, 0, gw // 2)
+    per = gw // GROUPS
+    band = lax.rem(row, per) + dr
     col = lax.broadcasted_iota(jnp.int32, off.shape, 2) + (off - 3 * dr) - 1
     left, right = col < 0, col >= gt
     side = left | right
-    rows = gw // 2 + 2
+    rows = per + 2
     local = jnp.where(side, bank * rows * gt, kind * (rows * gt) + band * gt + col)
     pack = LANES // gt
     for n in range(off.shape[0]):
@@ -130,17 +131,17 @@
             ref[start : start + count] = part[low : low + count]
 
 
-def local_kernel(dims, index_ref, x_ref, near_ref, far_ref, bank, out_ref, *scratch):
-    gw, gt, entries, unrolled = dims
-    index, top, low, sem = scratch
+def local_kernel(dims, index_ref, x_ref, near_ref, far_ref, bank, out_ref, index, *scratch):
+    gw, gt, entries = dims
+    tables, sem = scratch[:-1], scratch[-1]
     pack = LANES // gt
     even = lax.rem(lax.axis_index("weld"), 2) == 0
-    half, kernels = gw // 2, bank.shape[0]
-    step = (half + 2) * gt
+    per, kernels = gw // GROUPS, bank.shape[0]
+    step = (per + 2) * gt
     fetch = pltpu.make_async_copy(index_ref.at[: entries // pack], index, sem)
     fetch.start()
-    blank(top)
-    blank(low)
+    for table in tables:
+        blank(table)
     before = jnp.where(even, far_ref[...], near_ref[...])
     after = jnp.where(even, near_ref[...], far_ref[...])
 
@@ -151,33 +152,28 @@
         ]
         out_ref[r * gt + c] = tree(terms).astype(out_ref.dtype)
 
-    upper = [(top, step, 0, 0, step), (low, step, 0, half * gt, 2 * gt)]
-    lower = [(low, step, 2 * gt, 0, half * gt)]
-    cut = (half + 1) * gt
-    first = jnp.concatenate([before, x_ref[:cut]], axis=0).reshape(step * 16, 128)
-    for j in range(0, kernels, 2):
-        products(first, bank, j, upper)
-    fetch.wait()
-    second = jnp.concatenate([x_ref[cut:], after], axis=0).reshape(half * gt * 16, 128)
-    cells = [(r, c) for r in range(half) for c in range(gt)]
-    share = len(cells) * 2 // kernels
-    for j in range(0, kernels, 2):
-        products(second, bank, j, lower)
-        if unrolled:
+    share = per * gt * 2 // kernels
+    for g, table in enumerate(tables):
+        low, high = (0 if g == 0 else g * per + 2), g * per + per + 2
+        parts = [before] if low == 0 else []
+        parts.append(x_ref[max(low - 1, 0) * gt : min(high - 1, gw) * gt])
+        if high == gw + 2:
+            parts.append(after)
+        rows = jnp.concatenate(parts, axis=0) if len(parts) > 1 else parts[0]
+        fresh = (high - low) * gt
+        targets = [(table, step, step - fresh, 0, fresh)]
+        if g + 1 < GROUPS:
+            targets.append((tables[g + 1], step, 0, fresh - 2 * gt, 2 * gt))
+        cells = [((g - 1) * per + i // gt, i % gt) for i in range(per * gt)] if g else []
+        for j in range(0, kernels, 2):
+            products(rows.reshape(fresh * 16, 128), bank, j, targets)
             for r, c in cells[j // 2 * share : (j // 2 + 1) * share]:
-                gather(top, r, c)
-
-    def body(r, _, table):
+                gather(tables[g - 1], r, c)
+        if g == 0:
+            fetch.wait()
+    for r in range(gw - per, gw):
         for c in range(gt):
-            gather(table, r, c)
-        return 0
-
-    if unrolled:
-        for r in range(half, gw):
-            body(r, 0, low)
-    else:
-        lax.fori_loop(0, half, functools.partial(body, table=top), 0)
-        lax.fori_loop(half, gw, functools.partial(body, table=low), 0)
+            gather(tables[-1], r, c)
 
 
 def finish_kernel(dims, index_ref, *refs):
@@ -185,6 +181,7 @@
     own_ref = refs[0]
     count = peers - 1 + (0 if merged else 2)
     got = refs[1 : 1 + count]
+    got = got[: peers - 1][::-1] + got[peers - 1 :]
     bank_ref, wall_bank_ref, local_ref, rates_ref, walls_ref = refs[1 + count : 6 + count]
     index, table_ref, wall_table_ref, cols_ref, done_ref, sem = refs[6 + count :]
     fetch = pltpu.make_async_copy(index_ref.at[index_ref.shape[0] - 1], index, sem.at[0])
@@ -324,26 +321,25 @@
         if k:
             got[k] = lax.ppermute(message, "trans", [(i, i ^ k) for i in range(peers)])
     own = late_out[late.index(0)]
-    received = [got[k] for k in range(1, peers)]
+    received = [got[k] for k in range(peers - 1, 0, -1)]
     if not merged:
         received += [
             lax.ppermute(late_out[len(late) + s], "trans", pairing(peers, s)) for s in range(2)
         ]
 
-    step = (gw // 2 + 2) * gt
+    step = (gw // GROUPS + 2) * gt
     rates = pl.pallas_call(
-        functools.partial(local_kernel, (gw, gt, entries, UNROLLED)),
+        functools.partial(local_kernel, (gw, gt, entries)),
         name="local_pairs",
         out_shape=stack(total),
         in_specs=[HBM] + [VMEM] * 4,
         out_specs=VMEM,
         scratch_shapes=[
             pltpu.SMEM((planes - 1, gw, LANES), i32),
-            buffer(bank * step + 1),
-            buffer(bank * step + 1),
+            *[buffer(bank * step + 1)] * GROUPS,
             pltpu.SemaphoreType.DMA,
         ],
-        compiler_params=pltpu.CompilerParams(vmem_limit_bytes=44 * MIB),
+        compiler_params=pltpu.CompilerParams(vmem_limit_bytes=48 * MIB),
         cost_estimate=cost(2 * (gw + 2) * gt * channels * tile * tile * bank, 30),
     )(index, tiles, near, far, kernels)
 

time: 26.9 us -> 26.7 us (level)
  no operation moved by 1% of the time
where the time goes in v4:
time: 26.7 us; the launch traced here: 26.5 us
  Pallas kernels  14.5 us (54%)
  starting transfers between devices  11.2 us (42%)
  between operations  0.74 us (3%)
    pallas_call x1, Pallas kernels, on_device(): pl.pallas_call(functools.partial(local_kernel, (gw, gt, entries)), name='...  7.25 us
    ppermute x3, starting transfers between devices, on_device(): got[k] = lax.ppermute(message, 'trans', [(i, i ^ k) for i in range(peers)])  6.64 us
    ppermute x1, starting transfers between devices, on_device(): far = lax.ppermute(far_out, 'weld', pairing(weld, 1))  4.46 us
    pallas_call x1, Pallas kernels, on_device(): pl.pallas_call(functools.partial(finish_kernel, (gw, gt, entries, peers,...  2.64 us
    pallas_call x1, Pallas kernels, on_device(): pl.pallas_call(functools.partial(first_kernel, (gw, gt), early), name='ed...  2.23 us
    pallas_call x1, Pallas kernels, on_device(): pl.pallas_call(functools.partial(index_kernel, (gw, gt, bank, wall_bank,...  1.57 us
    pallas_call x1, Pallas kernels, on_device(): pl.pallas_call(functools.partial(second_kernel, (gw, gt, cap), late, merg...  0.84 us
  transfers between devices with their start and end apart: 5, of which 0 were waited for; matrix products, arithmetic and copies ran while one was open for 0% of the time, Pallas kernels for 36%

profile of v4, /device:TPU:1, one launch (start us, length us, event | category | flops | bytes accessed | tf_op | source)
XLA Modules:
  0.0 26.5 jit_solution(4158176448056331264)
XLA Ops:
  0.6 0.0 copy-start
  0.6 2.2 %edge_rows.1 = (bf16[32,16,128]{2,1,0:T(8,128)(2,1)}, bf16[32,16,128]{2,1,0:T(8,128)(2,1)}, bf16[32,16,128]{2,1,0:T(8,128)(2,1)}) custom-call(s32[4,32]{1,0:T(4,128)} %bitcast.12, bf16[256,16,128]{2,1,0:T(8,128)(2,1)} %bitcast.8), custom_call_target="tpu_custom_call" | custom-call | bytes 2097152 | tf_op jit(solution)/shard_map/edge_rows/pallas_call | solution.py:273
  2.9 0.1 collective-permute-start
  3.0 4.5 %collective-permute-start.1 = (bf16[32,16,128]{2,1,0:T(8,128)(2,1)}, bf16[32,16,128]{2,1,0:T(8,128)(2,1)S(1)}, u32[]{:S(2)}, u32[]{:S(2)}) collective-permute-start(bf16[32,16,128]{2,1,0:T(8,128)(2,1)} %get-tuple-element.11), channel_id=1, source_target_pairs={{4,8},{8,4},{12,16},{16,12},{20,24},{24,20},{5,9},{9,5},{13,17},{1... | collective-permute-start | bytes 393224 | tf_op jit(solution)/shard_map/ppermute | solution.py:288
  7.5 2.4 %collective-permute-start.3 = (bf16[32,16,128]{2,1,0:T(8,128)(2,1)}, bf16[32,16,128]{2,1,0:T(8,128)(2,1)S(1)}, u32[]{:S(2)}, u32[]{:S(2)}) collective-permute-start(bf16[32,16,128]{2,1,0:T(8,128)(2,1)} %get-tuple-element.14), channel_id=1, source_target_pairs={{0,2},{1,3},{2,0},{3,1},{4,6},{5,7},{6,4},{7,5},{8,10},{9,11},{10,... | collective-permute-start | bytes 393224 | tf_op jit(solution)/shard_map/ppermute | solution.py:291
  9.8 0.0 copy-start.4
  9.8 1.6 %pair_index.1.index_ref = s32[4,8,128]{2,1,0:T(8,128)} custom-call(s32[12,8,32]{2,1,0:T(8,128)} %bitcast.14, s32[12,8,32]{2,1,0:T(8,128)} %bitcast.15, s32[16,16]{1,0:T(8,128)} %bitcast.16, s32[16,16]{1,0:T(8,128)} %bitcast.17), custom_call_target="tpu_custom_call" | custom-call | flops 1000000 | bytes 3145728 | tf_op jit(solution)/shard_map/pair_index/pallas_call | solution.py:294
  11.4 0.0 copy-start.1
  11.4 0.0 copy-start.3
  11.4 0.0 collective-permute-done.near_ref
  11.4 0.0 collective-permute-done.1.far_ref
  11.4 0.0 copy-done
  11.4 0.0 copy-done.4
  11.5 0.8 %edge_columns.1 = (bf16[42,16,128]{2,1,0:T(8,128)(2,1)S(1)}, bf16[42,16,128]{2,1,0:T(8,128)(2,1)S(1)}, bf16[32,16,128]{2,1,0:T(8,128)(2,1)S(1)}) custom-call(s32[4,32]{1,0:T(4,128)S(1)} %bitcast.13, bf16[256,16,128]{2,1,0:T(8,128)(2,1)S(1)} %bitcast.9, bf16[32,16,128]{2,1,0:T(8,128)(2,1)S(1)} %collective-permute-done.near_ref, ...), custom_call_target="tpu_custom_call" | custom-call | bytes 2097152 | tf_op jit(solution)/shard_map/edge_columns/pallas_call | solution.py:311
  12.3 4.3 %collective-permute-start.2 = (bf16[42,16,128]{2,1,0:T(8,128)(2,1)S(1)}, bf16[42,16,128]{2,1,0:T(8,128)(2,1)S(1)}, u32[]{:S(2)}, u32[]{:S(2)}) collective-permute-start(bf16[42,16,128]{2,1,0:T(8,128)(2,1)S(1)} %get-tuple-element.13), channel_id=1, source_target_pairs={{0,3},{1,2},{2,1},{3,0},{4,7},{5,6},{6,5},{7,4},{8,11},{9,10},{10,... | collective-permute-start | bytes 516104 | tf_op jit(solution)/shard_map/ppermute | solution.py:322
  16.6 0.0 copy-start.2
  16.6 0.0 collective-permute-start.4
  16.6 0.0 copy-done.1
  16.6 0.0 copy-done.3
  16.6 7.3 %local_pairs.1 = bf16[256,16,128]{2,1,0:T(8,128)(2,1)S(1)} custom-call(s32[4,8,128]{2,1,0:T(8,128)S(1)} %copy-done.3, bf16[256,16,128]{2,1,0:T(8,128)(2,1)S(1)} %bitcast.10, bf16[32,16,128]{2,1,0:T(8,128)(2,1)S(1)} %collective-permute-done.near_ref, bf16[32,16,128]{2,1,0:T(8,128)(2,1)S(1)} %collective-permute-done.1.far_ref, bf16[16,128,128]{2,1,0:T(8,128)(2,1)S(1)} %copy-done.1), custom_call_target="tpu_custom_call" | custom-call | flops 2684354560 | bytes 31457280 | tf_op jit(solution)/shard_map/local_pairs/pallas_call | solution.py:331
  23.8 0.0 collective-permute-done.3.refs_2_
  23.9 0.0 collective-permute-done.2.refs_1_
  23.9 0.0 collective-permute-done.4.refs_3_
  23.9 0.0 copy-done.2
  23.9 2.6 %columns_and_walls.1 = (bf16[8,32,16,128]{3,2,1,0:T(8,128)(2,1)}, bf16[16,16,128]{2,1,0:T(8,128)(2,1)}) custom-call(s32[4,8,128]{2,1,0:T(8,128)S(1)} %copy-done.3, bf16[32,16,128]{2,1,0:T(8,128)(2,1)S(1)} %get-tuple-element.12.refs_0_, bf16[42,16,128]{2,1,0:T(8,128)(2,1)S(1)} %collective-permute-done.2.refs_1_, ...), custom_call_target="tpu_custom_call" | custom-call | flops 536870912 | bytes 8388608 | tf_op jit(solution)/shard_map/columns_and_walls/pallas_call | solution.py:347
Async XLA Ops:
  0.6 10.8 %copy-start = (bf16[8,32,16,128]{3,2,1,0:T(8,128)(2,1)S(1)}, bf16[8,32,16,128]{3,2,1,0:T(8,128)(2,1)}, u32[]{:S(2)}) copy-start(bf16[8,32,16,128]{3,2,1,0:T(8,128)(2,1)} %param.8) | copy-start | bytes 3145732
  2.9 8.5 %collective-permute-start = (bf16[32,16,128]{2,1,0:T(8,128)(2,1)}, bf16[32,16,128]{2,1,0:T(8,128)(2,1)S(1)}, u32[]{:S(2)}, u32[]{:S(2)}) collective-permute-start(bf16[32,16,128]{2,1,0:T(8,128)(2,1)} %get-tuple-element.10), channel_id=1, source_target_pairs={{0,4},{4,0},{8,12},{12,8},{16,20},{20,16},{24,28},{28,24},{1,5},{5... | collective-permute-start | bytes 393224 | tf_op jit(solution)/shard_map/ppermute | solution.py:287
  3.0 8.4 %collective-permute-start.1 = (bf16[32,16,128]{2,1,0:T(8,128)(2,1)}, bf16[32,16,128]{2,1,0:T(8,128)(2,1)S(1)}, u32[]{:S(2)}, u32[]{:S(2)}) collective-permute-start(bf16[32,16,128]{2,1,0:T(8,128)(2,1)} %get-tuple-element.11), channel_id=1, source_target_pairs={{4,8},{8,4},{12,16},{16,12},{20,24},{24,20},{5,9},{9,5},{13,17},{1... | collective-permute-start | bytes 393224 | tf_op jit(solution)/shard_map/ppermute | solution.py:288
  7.5 16.4 %collective-permute-start.3 = (bf16[32,16,128]{2,1,0:T(8,128)(2,1)}, bf16[32,16,128]{2,1,0:T(8,128)(2,1)S(1)}, u32[]{:S(2)}, u32[]{:S(2)}) collective-permute-start(bf16[32,16,128]{2,1,0:T(8,128)(2,1)} %get-tuple-element.14), channel_id=1, source_target_pairs={{0,2},{1,3},{2,0},{3,1},{4,6},{5,7},{6,4},{7,5},{8,10},{9,11},{10,... | collective-permute-start | bytes 393224 | tf_op jit(solution)/shard_map/ppermute | solution.py:291
  9.8 1.6 %copy-start.4 = (s32[1,1,4,32]{3,2,1,0:T(4,128)S(1)}, s32[1,1,4,32]{3,2,1,0:T(4,128)}, u32[]{:S(2)}) copy-start(s32[1,1,4,32]{3,2,1,0:T(4,128)} %param.12) | copy-start | bytes 1540
  11.4 5.2 %copy-start.1 = (bf16[16,128,128]{2,1,0:T(8,128)(2,1)S(1)}, bf16[16,128,128]{2,1,0:T(8,128)(2,1)}, u32[]{:S(2)}) copy-start(bf16[16,128,128]{2,1,0:T(8,128)(2,1)} %refs_4_.1) | copy-start | bytes 1572868
  11.4 5.2 %copy-start.3 = (s32[4,8,128]{2,1,0:T(8,128)S(1)}, s32[4,8,128]{2,1,0:T(8,128)}, u32[]{:S(2)}) copy-start(s32[4,8,128]{2,1,0:T(8,128)} %pair_index.1.index_ref) | copy-start | bytes 49156
  12.3 11.6 %collective-permute-start.2 = (bf16[42,16,128]{2,1,0:T(8,128)(2,1)S(1)}, bf16[42,16,128]{2,1,0:T(8,128)(2,1)S(1)}, u32[]{:S(2)}, u32[]{:S(2)}) collective-permute-start(bf16[42,16,128]{2,1,0:T(8,128)(2,1)S(1)} %get-tuple-element.13), channel_id=1, source_target_pairs={{0,3},{1,2},{2,1},{3,0},{4,7},{5,6},{6,5},{7,4},{8,11},{9,10},{10,... | collective-permute-start | bytes 516104 | tf_op jit(solution)/shard_map/ppermute | solution.py:322
  16.6 7.3 %copy-start.2 = (bf16[8,128,128]{2,1,0:T(8,128)(2,1)S(1)}, bf16[8,128,128]{2,1,0:T(8,128)(2,1)}, u32[]{:S(2)}) copy-start(bf16[8,128,128]{2,1,0:T(8,128)(2,1)} %refs_5_.1) | copy-start | bytes 786436
  16.6 7.3 %collective-permute-start.4 = (bf16[42,16,128]{2,1,0:T(8,128)(2,1)S(1)}, bf16[42,16,128]{2,1,0:T(8,128)(2,1)S(1)}, u32[]{:S(2)}, u32[]{:S(2)}) collective-permute-start(bf16[42,16,128]{2,1,0:T(8,128)(2,1)S(1)} %get-tuple-element.15), channel_id=1, source_target_pairs={{0,1},{1,0},{2,3},{3,2},{4,5},{5,4},{6,7},{7,6},{8,9},{9,8},{10,11... | collective-permute-start | bytes 516104 | tf_op jit(solution)/shard_map/ppermute | solution.py:322

commit v5 on v4

--- a/solution.py
+++ b/solution.py
@@ -79,19 +79,20 @@
     def span(first, count):
         return pl.ds(first * gt, count * gt)
 
+    half = gw // 2
     loads = [
-        pltpu.make_async_copy(x_ref.at[at], held_ref.at[at], sem.at[i])
-        for i, at in enumerate((span(0, 1), span(gw - 1, 1), span(1, gw - 2)))
+        pltpu.make_async_copy(list_ref, picks_ref, sem.at[0]),
+        pltpu.make_async_copy(x_ref.at[span(0, half)], held_ref.at[span(0, half)], sem.at[1]),
+        pltpu.make_async_copy(
+            x_ref.at[span(half, half)], held_ref.at[span(half, half)], sem.at[2]
+        ),
     ]
-    loads.append(pltpu.make_async_copy(list_ref, picks_ref, sem.at[5]))
     for copy in loads:
         copy.start()
-    loads[0].wait()
-    loads[1].wait()
+    for copy in loads:
+        copy.wait()
     near_ref[...] = held_ref[span(pick(even, gw - 1, 0), 1)]
     far_ref[...] = held_ref[span(pick(even, 0, gw - 1), 1)]
-    loads[2].wait()
-    loads[3].wait()
     for k, ref in zip(early, outs):
         listed(held_ref, gw * gt, picks_ref, t ^ k, ref)
 
@@ -279,7 +280,7 @@
         scratch_shapes=[
             pltpu.SMEM((peers, cap), i32),
             buffer(total),
-            pltpu.SemaphoreType.DMA((6,)),
+            pltpu.SemaphoreType.DMA((3,)),
         ],
         compiler_params=pltpu.CompilerParams(vmem_limit_bytes=56 * MIB),
         cost_estimate=cost(0, 2),

time: 26.7 us -> 26.6 us (level)
  transfers between devices with their start and end apart: 5 -> 5, of which waited for: 0 -> 0; matrix products, arithmetic and copies ran while one was open for 0% -> 0% of each run, Pallas kernels for 36% -> 37%
where the time goes in v5:
time: 26.6 us; the launch traced here: 26.4 us
  Pallas kernels  14.4 us (54%)
  starting transfers between devices  11.2 us (42%)
  between operations  0.74 us (3%)
    pallas_call x1, Pallas kernels, on_device(): pl.pallas_call(functools.partial(local_kernel, (gw, gt, entries)), name='...  7.25 us
    ppermute x3, starting transfers between devices, on_device(): got[k] = lax.ppermute(message, 'trans', [(i, i ^ k) for i in range(peers)])  6.64 us
    ppermute x1, starting transfers between devices, on_device(): far = lax.ppermute(far_out, 'weld', pairing(weld, 1))  4.46 us
    pallas_call x1, Pallas kernels, on_device(): pl.pallas_call(functools.partial(finish_kernel, (gw, gt, entries, peers,...  2.64 us
    pallas_call x1, Pallas kernels, on_device(): pl.pallas_call(functools.partial(first_kernel, (gw, gt), early), name='ed...  2.13 us
    pallas_call x1, Pallas kernels, on_device(): pl.pallas_call(functools.partial(index_kernel, (gw, gt, bank, wall_bank,...  1.57 us
    pallas_call x1, Pallas kernels, on_device(): pl.pallas_call(functools.partial(second_kernel, (gw, gt, cap), late, merg...  0.84 us
  transfers between devices with their start and end apart: 5, of which 0 were waited for; matrix products, arithmetic and copies ran while one was open for 0% of the time, Pallas kernels for 37%

profile of v5, /device:TPU:1, one launch (start us, length us, event | category | flops | bytes accessed | tf_op | source)
XLA Modules:
  0.0 26.4 jit_solution(6164034803133925794)
XLA Ops:
  0.6 0.0 copy-start
  0.6 2.1 %edge_rows.1 = (bf16[32,16,128]{2,1,0:T(8,128)(2,1)}, bf16[32,16,128]{2,1,0:T(8,128)(2,1)}, bf16[32,16,128]{2,1,0:T(8,128)(2,1)}) custom-call(s32[4,32]{1,0:T(4,128)} %bitcast.12, bf16[256,16,128]{2,1,0:T(8,128)(2,1)} %bitcast.8), custom_call_target="tpu_custom_call" | custom-call | bytes 2097152 | tf_op jit(solution)/shard_map/edge_rows/pallas_call | solution.py:274
  2.8 0.1 collective-permute-start
  2.9 4.5 %collective-permute-start.1 = (bf16[32,16,128]{2,1,0:T(8,128)(2,1)}, bf16[32,16,128]{2,1,0:T(8,128)(2,1)S(1)}, u32[]{:S(2)}, u32[]{:S(2)}) collective-permute-start(bf16[32,16,128]{2,1,0:T(8,128)(2,1)} %get-tuple-element.11), channel_id=1, source_target_pairs={{4,8},{8,4},{12,16},{16,12},{20,24},{24,20},{5,9},{9,5},{13,17},{1... | collective-permute-start | bytes 393224 | tf_op jit(solution)/shard_map/ppermute | solution.py:289
  7.4 2.4 %collective-permute-start.3 = (bf16[32,16,128]{2,1,0:T(8,128)(2,1)}, bf16[32,16,128]{2,1,0:T(8,128)(2,1)S(1)}, u32[]{:S(2)}, u32[]{:S(2)}) collective-permute-start(bf16[32,16,128]{2,1,0:T(8,128)(2,1)} %get-tuple-element.14), channel_id=1, source_target_pairs={{0,2},{1,3},{2,0},{3,1},{4,6},{5,7},{6,4},{7,5},{8,10},{9,11},{10,... | collective-permute-start | bytes 393224 | tf_op jit(solution)/shard_map/ppermute | solution.py:292
  9.8 0.0 copy-start.4
  9.8 1.6 %pair_index.1.index_ref = s32[4,8,128]{2,1,0:T(8,128)} custom-call(s32[12,8,32]{2,1,0:T(8,128)} %bitcast.14, s32[12,8,32]{2,1,0:T(8,128)} %bitcast.15, s32[16,16]{1,0:T(8,128)} %bitcast.16, s32[16,16]{1,0:T(8,128)} %bitcast.17), custom_call_target="tpu_custom_call" | custom-call | flops 1000000 | bytes 3145728 | tf_op jit(solution)/shard_map/pair_index/pallas_call | solution.py:295
  11.3 0.0 copy-start.1
  11.3 0.0 copy-start.3
  11.3 0.0 collective-permute-done.near_ref
  11.3 0.0 collective-permute-done.1.far_ref
  11.3 0.0 copy-done
  11.4 0.0 copy-done.4
  11.4 0.8 %edge_columns.1 = (bf16[42,16,128]{2,1,0:T(8,128)(2,1)S(1)}, bf16[42,16,128]{2,1,0:T(8,128)(2,1)S(1)}, bf16[32,16,128]{2,1,0:T(8,128)(2,1)S(1)}) custom-call(s32[4,32]{1,0:T(4,128)S(1)} %bitcast.13, bf16[256,16,128]{2,1,0:T(8,128)(2,1)S(1)} %bitcast.9, bf16[32,16,128]{2,1,0:T(8,128)(2,1)S(1)} %collective-permute-done.near_ref, ...), custom_call_target="tpu_custom_call" | custom-call | bytes 2097152 | tf_op jit(solution)/shard_map/edge_columns/pallas_call | solution.py:312
  12.2 4.3 %collective-permute-start.2 = (bf16[42,16,128]{2,1,0:T(8,128)(2,1)S(1)}, bf16[42,16,128]{2,1,0:T(8,128)(2,1)S(1)}, u32[]{:S(2)}, u32[]{:S(2)}) collective-permute-start(bf16[42,16,128]{2,1,0:T(8,128)(2,1)S(1)} %get-tuple-element.13), channel_id=1, source_target_pairs={{0,3},{1,2},{2,1},{3,0},{4,7},{5,6},{6,5},{7,4},{8,11},{9,10},{10,... | collective-permute-start | bytes 516104 | tf_op jit(solution)/shard_map/ppermute | solution.py:323
  16.5 0.0 copy-start.2
  16.5 0.0 collective-permute-start.4
  16.5 0.0 copy-done.1
  16.5 0.0 copy-done.3
  16.5 7.2 %local_pairs.1 = bf16[256,16,128]{2,1,0:T(8,128)(2,1)S(1)} custom-call(s32[4,8,128]{2,1,0:T(8,128)S(1)} %copy-done.3, bf16[256,16,128]{2,1,0:T(8,128)(2,1)S(1)} %bitcast.10, bf16[32,16,128]{2,1,0:T(8,128)(2,1)S(1)} %collective-permute-done.near_ref, bf16[32,16,128]{2,1,0:T(8,128)(2,1)S(1)} %collective-permute-done.1.far_ref, bf16[16,128,128]{2,1,0:T(8,128)(2,1)S(1)} %copy-done.1), custom_call_target="tpu_custom_call" | custom-call | flops 2684354560 | bytes 31457280 | tf_op jit(solution)/shard_map/local_pairs/pallas_call | solution.py:332
  23.7 0.0 collective-permute-done.3.refs_2_
  23.8 0.0 collective-permute-done.2.refs_1_
  23.8 0.0 collective-permute-done.4.refs_3_
  23.8 0.0 copy-done.2
  23.8 2.6 %columns_and_walls.1 = (bf16[8,32,16,128]{3,2,1,0:T(8,128)(2,1)}, bf16[16,16,128]{2,1,0:T(8,128)(2,1)}) custom-call(s32[4,8,128]{2,1,0:T(8,128)S(1)} %copy-done.3, bf16[32,16,128]{2,1,0:T(8,128)(2,1)S(1)} %get-tuple-element.12.refs_0_, bf16[42,16,128]{2,1,0:T(8,128)(2,1)S(1)} %collective-permute-done.2.refs_1_, ...), custom_call_target="tpu_custom_call" | custom-call | flops 536870912 | bytes 8388608 | tf_op jit(solution)/shard_map/columns_and_walls/pallas_call | solution.py:348
Async XLA Ops:
  0.6 10.7 %copy-start = (bf16[8,32,16,128]{3,2,1,0:T(8,128)(2,1)S(1)}, bf16[8,32,16,128]{3,2,1,0:T(8,128)(2,1)}, u32[]{:S(2)}) copy-start(bf16[8,32,16,128]{3,2,1,0:T(8,128)(2,1)} %param.8) | copy-start | bytes 3145732
  2.8 8.5 %collective-permute-start = (bf16[32,16,128]{2,1,0:T(8,128)(2,1)}, bf16[32,16,128]{2,1,0:T(8,128)(2,1)S(1)}, u32[]{:S(2)}, u32[]{:S(2)}) collective-permute-start(bf16[32,16,128]{2,1,0:T(8,128)(2,1)} %get-tuple-element.10), channel_id=1, source_target_pairs={{0,4},{4,0},{8,12},{12,8},{16,20},{20,16},{24,28},{28,24},{1,5},{5... | collective-permute-start | bytes 393224 | tf_op jit(solution)/shard_map/ppermute | solution.py:288
  2.9 8.4 %collective-permute-start.1 = (bf16[32,16,128]{2,1,0:T(8,128)(2,1)}, bf16[32,16,128]{2,1,0:T(8,128)(2,1)S(1)}, u32[]{:S(2)}, u32[]{:S(2)}) collective-permute-start(bf16[32,16,128]{2,1,0:T(8,128)(2,1)} %get-tuple-element.11), channel_id=1, source_target_pairs={{4,8},{8,4},{12,16},{16,12},{20,24},{24,20},{5,9},{9,5},{13,17},{1... | collective-permute-start | bytes 393224 | tf_op jit(solution)/shard_map/ppermute | solution.py:289
  7.4 16.4 %collective-permute-start.3 = (bf16[32,16,128]{2,1,0:T(8,128)(2,1)}, bf16[32,16,128]{2,1,0:T(8,128)(2,1)S(1)}, u32[]{:S(2)}, u32[]{:S(2)}) collective-permute-start(bf16[32,16,128]{2,1,0:T(8,128)(2,1)} %get-tuple-element.14), channel_id=1, source_target_pairs={{0,2},{1,3},{2,0},{3,1},{4,6},{5,7},{6,4},{7,5},{8,10},{9,11},{10,... | collective-permute-start | bytes 393224 | tf_op jit(solution)/shard_map/ppermute | solution.py:292
  9.8 1.6 %copy-start.4 = (s32[1,1,4,32]{3,2,1,0:T(4,128)S(1)}, s32[1,1,4,32]{3,2,1,0:T(4,128)}, u32[]{:S(2)}) copy-start(s32[1,1,4,32]{3,2,1,0:T(4,128)} %param.12) | copy-start | bytes 1540
  11.3 5.2 %copy-start.1 = (bf16[16,128,128]{2,1,0:T(8,128)(2,1)S(1)}, bf16[16,128,128]{2,1,0:T(8,128)(2,1)}, u32[]{:S(2)}) copy-start(bf16[16,128,128]{2,1,0:T(8,128)(2,1)} %refs_4_.1) | copy-start | bytes 1572868
  11.3 5.2 %copy-start.3 = (s32[4,8,128]{2,1,0:T(8,128)S(1)}, s32[4,8,128]{2,1,0:T(8,128)}, u32[]{:S(2)}) copy-start(s32[4,8,128]{2,1,0:T(8,128)} %pair_index.1.index_ref) | copy-start | bytes 49156
  12.2 11.5 %collective-permute-start.2 = (bf16[42,16,128]{2,1,0:T(8,128)(2,1)S(1)}, bf16[42,16,128]{2,1,0:T(8,128)(2,1)S(1)}, u32[]{:S(2)}, u32[]{:S(2)}) collective-permute-start(bf16[42,16,128]{2,1,0:T(8,128)(2,1)S(1)} %get-tuple-element.13), channel_id=1, source_target_pairs={{0,3},{1,2},{2,1},{3,0},{4,7},{5,6},{6,5},{7,4},{8,11},{9,10},{10,... | collective-permute-start | bytes 516104 | tf_op jit(solution)/shard_map/ppermute | solution.py:323
  16.5 7.3 %copy-start.2 = (bf16[8,128,128]{2,1,0:T(8,128)(2,1)S(1)}, bf16[8,128,128]{2,1,0:T(8,128)(2,1)}, u32[]{:S(2)}) copy-start(bf16[8,128,128]{2,1,0:T(8,128)(2,1)} %refs_5_.1) | copy-start | bytes 786436
  16.5 7.3 %collective-permute-start.4 = (bf16[42,16,128]{2,1,0:T(8,128)(2,1)S(1)}, bf16[42,16,128]{2,1,0:T(8,128)(2,1)S(1)}, u32[]{:S(2)}, u32[]{:S(2)}) collective-permute-start(bf16[42,16,128]{2,1,0:T(8,128)(2,1)S(1)} %get-tuple-element.15), channel_id=1, source_target_pairs={{0,1},{1,0},{2,3},{3,2},{4,5},{5,4},{6,7},{7,6},{8,9},{9,8},{10,11... | collective-permute-start | bytes 516104 | tf_op jit(solution)/shard_map/ppermute | solution.py:323

commit v6 on v5

--- a/solution.py
+++ b/solution.py
@@ -209,14 +209,14 @@
         sides = [got[-2][...], got[-1][...]]
     blank(table_ref)
     blank(wall_table_ref)
-    ring = jnp.concatenate(sides, axis=0).reshape(2 * depth * 16, 128)
-    for j in range(0, bank_ref.shape[0], 2):
-        products(ring, bank_ref, j, [(table_ref, 2 * depth, 0, 0, 2 * depth)])
     slots = peers * cap
     received = jnp.concatenate([own_ref[...]] + [g[:cap] for g in got[: peers - 1]], axis=0)
     received = received.reshape(slots * 16, 128)
     for j in range(0, wall_bank_ref.shape[0], 2):
         products(received, wall_bank_ref, j, [(wall_table_ref, slots, 0, 0, slots)])
+    ring = jnp.concatenate(sides, axis=0).reshape(2 * depth * 16, 128)
+    for j in range(0, bank_ref.shape[0], 2):
+        products(ring, bank_ref, j, [(table_ref, 2 * depth, 0, 0, 2 * depth)])
     fetch.wait()
     for e, c in enumerate((0, gt - 1)):
         for r in range(gw):

time: 26.6 us -> 27 us (1.015)
  Pallas kernels: 14.4 us -> 14.8 us
    pallas_call x1, Pallas kernels: 2.64 us -> 2.96 us  [on_device(): pl.pallas_call(functools.partial(finish_kernel, (gw, gt, entries, peers,...]
  transfers between devices with their start and end apart: 5 -> 5, of which waited for: 0 -> 0; matrix products, arithmetic and copies ran while one was open for 0% -> 0% of each run, Pallas kernels for 37% -> 36%
where the time goes in v6:
time: 27 us; the launch traced here: 26.8 us
  Pallas kernels  14.8 us (55%)
  starting transfers between devices  11.2 us (41%)
  between operations  0.74 us (3%)
    pallas_call x1, Pallas kernels, on_device(): pl.pallas_call(functools.partial(local_kernel, (gw, gt, entries)), name='...  7.27 us
    ppermute x3, starting transfers between devices, on_device(): got[k] = lax.ppermute(message, 'trans', [(i, i ^ k) for i in range(peers)])  6.64 us
    ppermute x1, starting transfers between devices, on_device(): far = lax.ppermute(far_out, 'weld', pairing(weld, 1))  4.46 us
    pallas_call x1, Pallas kernels, on_device(): pl.pallas_call(functools.partial(finish_kernel, (gw, gt, entries, peers,...  2.96 us
    pallas_call x1, Pallas kernels, on_device(): pl.pallas_call(functools.partial(first_kernel, (gw, gt), early), name='ed...  2.13 us
    pallas_call x1, Pallas kernels, on_device(): pl.pallas_call(functools.partial(index_kernel, (gw, gt, bank, wall_bank,...  1.57 us
    pallas_call x1, Pallas kernels, on_device(): pl.pallas_call(functools.partial(second_kernel, (gw, gt, cap), late, merg...  0.84 us
  transfers between devices with their start and end apart: 5, of which 0 were waited for; matrix products, arithmetic and copies ran while one was open for 0% of the time, Pallas kernels for 36%

profile of v6, /device:TPU:1, one launch (start us, length us, event | category | flops | bytes accessed | tf_op | source)
XLA Modules:
  0.0 26.8 jit_solution(17918743786131415645)
XLA Ops:
  0.6 0.0 copy-start
  0.6 2.1 %edge_rows.1 = (bf16[32,16,128]{2,1,0:T(8,128)(2,1)}, bf16[32,16,128]{2,1,0:T(8,128)(2,1)}, bf16[32,16,128]{2,1,0:T(8,128)(2,1)}) custom-call(s32[4,32]{1,0:T(4,128)} %bitcast.12, bf16[256,16,128]{2,1,0:T(8,128)(2,1)} %bitcast.8), custom_call_target="tpu_custom_call" | custom-call | bytes 2097152 | tf_op jit(solution)/shard_map/edge_rows/pallas_call | solution.py:274
  2.8 0.1 collective-permute-start
  2.9 4.5 %collective-permute-start.1 = (bf16[32,16,128]{2,1,0:T(8,128)(2,1)}, bf16[32,16,128]{2,1,0:T(8,128)(2,1)S(1)}, u32[]{:S(2)}, u32[]{:S(2)}) collective-permute-start(bf16[32,16,128]{2,1,0:T(8,128)(2,1)} %get-tuple-element.11), channel_id=1, source_target_pairs={{4,8},{8,4},{12,16},{16,12},{20,24},{24,20},{5,9},{9,5},{13,17},{1... | collective-permute-start | bytes 393224 | tf_op jit(solution)/shard_map/ppermute | solution.py:289
  7.4 2.4 %collective-permute-start.3 = (bf16[32,16,128]{2,1,0:T(8,128)(2,1)}, bf16[32,16,128]{2,1,0:T(8,128)(2,1)S(1)}, u32[]{:S(2)}, u32[]{:S(2)}) collective-permute-start(bf16[32,16,128]{2,1,0:T(8,128)(2,1)} %get-tuple-element.14), channel_id=1, source_target_pairs={{0,2},{1,3},{2,0},{3,1},{4,6},{5,7},{6,4},{7,5},{8,10},{9,11},{10,... | collective-permute-start | bytes 393224 | tf_op jit(solution)/shard_map/ppermute | solution.py:292
  9.8 0.0 copy-start.4
  9.8 1.6 %pair_index.1.index_ref = s32[4,8,128]{2,1,0:T(8,128)} custom-call(s32[12,8,32]{2,1,0:T(8,128)} %bitcast.14, s32[12,8,32]{2,1,0:T(8,128)} %bitcast.15, s32[16,16]{1,0:T(8,128)} %bitcast.16, s32[16,16]{1,0:T(8,128)} %bitcast.17), custom_call_target="tpu_custom_call" | custom-call | flops 1000000 | bytes 3145728 | tf_op jit(solution)/shard_map/pair_index/pallas_call | solution.py:295
  11.3 0.0 copy-start.1
  11.3 0.0 copy-start.3
  11.3 0.0 collective-permute-done.near_ref
  11.3 0.0 collective-permute-done.1.far_ref
  11.3 0.0 copy-done
  11.4 0.0 copy-done.4
  11.4 0.8 %edge_columns.1 = (bf16[42,16,128]{2,1,0:T(8,128)(2,1)S(1)}, bf16[42,16,128]{2,1,0:T(8,128)(2,1)S(1)}, bf16[32,16,128]{2,1,0:T(8,128)(2,1)S(1)}) custom-call(s32[4,32]{1,0:T(4,128)S(1)} %bitcast.13, bf16[256,16,128]{2,1,0:T(8,128)(2,1)S(1)} %bitcast.9, bf16[32,16,128]{2,1,0:T(8,128)(2,1)S(1)} %collective-permute-done.near_ref, ...), custom_call_target="tpu_custom_call" | custom-call | bytes 2097152 | tf_op jit(solution)/shard_map/edge_columns/pallas_call | solution.py:312
  12.2 4.3 %collective-permute-start.2 = (bf16[42,16,128]{2,1,0:T(8,128)(2,1)S(1)}, bf16[42,16,128]{2,1,0:T(8,128)(2,1)S(1)}, u32[]{:S(2)}, u32[]{:S(2)}) collective-permute-start(bf16[42,16,128]{2,1,0:T(8,128)(2,1)S(1)} %get-tuple-element.13), channel_id=1, source_target_pairs={{0,3},{1,2},{2,1},{3,0},{4,7},{5,6},{6,5},{7,4},{8,11},{9,10},{10,... | collective-permute-start | bytes 516104 | tf_op jit(solution)/shard_map/ppermute | solution.py:323
  16.5 0.0 copy-start.2
  16.5 0.0 collective-permute-start.4
  16.5 0.0 copy-done.1
  16.5 0.0 copy-done.3
  16.5 7.3 %local_pairs.1 = bf16[256,16,128]{2,1,0:T(8,128)(2,1)S(1)} custom-call(s32[4,8,128]{2,1,0:T(8,128)S(1)} %copy-done.3, bf16[256,16,128]{2,1,0:T(8,128)(2,1)S(1)} %bitcast.10, bf16[32,16,128]{2,1,0:T(8,128)(2,1)S(1)} %collective-permute-done.near_ref, bf16[32,16,128]{2,1,0:T(8,128)(2,1)S(1)} %collective-permute-done.1.far_ref, bf16[16,128,128]{2,1,0:T(8,128)(2,1)S(1)} %copy-done.1), custom_call_target="tpu_custom_call" | custom-call | flops 2684354560 | bytes 31457280 | tf_op jit(solution)/shard_map/local_pairs/pallas_call | solution.py:332
  23.8 0.0 collective-permute-done.3.refs_2_
  23.8 0.0 collective-permute-done.2.refs_1_
  23.8 0.0 collective-permute-done.4.refs_3_
  23.8 0.0 copy-done.2
  23.8 3.0 %columns_and_walls.1 = (bf16[8,32,16,128]{3,2,1,0:T(8,128)(2,1)}, bf16[16,16,128]{2,1,0:T(8,128)(2,1)}) custom-call(s32[4,8,128]{2,1,0:T(8,128)S(1)} %copy-done.3, bf16[32,16,128]{2,1,0:T(8,128)(2,1)S(1)} %get-tuple-element.12.refs_0_, bf16[42,16,128]{2,1,0:T(8,128)(2,1)S(1)} %collective-permute-done.2.refs_1_, ...), custom_call_target="tpu_custom_call" | custom-call | flops 536870912 | bytes 8388608 | tf_op jit(solution)/shard_map/columns_and_walls/pallas_call | solution.py:348
Async XLA Ops:
  0.6 10.7 %copy-start = (bf16[8,32,16,128]{3,2,1,0:T(8,128)(2,1)S(1)}, bf16[8,32,16,128]{3,2,1,0:T(8,128)(2,1)}, u32[]{:S(2)}) copy-start(bf16[8,32,16,128]{3,2,1,0:T(8,128)(2,1)} %param.8) | copy-start | bytes 3145732
  2.8 8.5 %collective-permute-start = (bf16[32,16,128]{2,1,0:T(8,128)(2,1)}, bf16[32,16,128]{2,1,0:T(8,128)(2,1)S(1)}, u32[]{:S(2)}, u32[]{:S(2)}) collective-permute-start(bf16[32,16,128]{2,1,0:T(8,128)(2,1)} %get-tuple-element.10), channel_id=1, source_target_pairs={{0,4},{4,0},{8,12},{12,8},{16,20},{20,16},{24,28},{28,24},{1,5},{5... | collective-permute-start | bytes 393224 | tf_op jit(solution)/shard_map/ppermute | solution.py:288
  2.9 8.4 %collective-permute-start.1 = (bf16[32,16,128]{2,1,0:T(8,128)(2,1)}, bf16[32,16,128]{2,1,0:T(8,128)(2,1)S(1)}, u32[]{:S(2)}, u32[]{:S(2)}) collective-permute-start(bf16[32,16,128]{2,1,0:T(8,128)(2,1)} %get-tuple-element.11), channel_id=1, source_target_pairs={{4,8},{8,4},{12,16},{16,12},{20,24},{24,20},{5,9},{9,5},{13,17},{1... | collective-permute-start | bytes 393224 | tf_op jit(solution)/shard_map/ppermute | solution.py:289
  7.4 16.4 %collective-permute-start.3 = (bf16[32,16,128]{2,1,0:T(8,128)(2,1)}, bf16[32,16,128]{2,1,0:T(8,128)(2,1)S(1)}, u32[]{:S(2)}, u32[]{:S(2)}) collective-permute-start(bf16[32,16,128]{2,1,0:T(8,128)(2,1)} %get-tuple-element.14), channel_id=1, source_target_pairs={{0,2},{1,3},{2,0},{3,1},{4,6},{5,7},{6,4},{7,5},{8,10},{9,11},{10,... | collective-permute-start | bytes 393224 | tf_op jit(solution)/shard_map/ppermute | solution.py:292
  9.8 1.6 %copy-start.4 = (s32[1,1,4,32]{3,2,1,0:T(4,128)S(1)}, s32[1,1,4,32]{3,2,1,0:T(4,128)}, u32[]{:S(2)}) copy-start(s32[1,1,4,32]{3,2,1,0:T(4,128)} %param.12) | copy-start | bytes 1540
  11.3 5.2 %copy-start.1 = (bf16[16,128,128]{2,1,0:T(8,128)(2,1)S(1)}, bf16[16,128,128]{2,1,0:T(8,128)(2,1)}, u32[]{:S(2)}) copy-start(bf16[16,128,128]{2,1,0:T(8,128)(2,1)} %refs_4_.1) | copy-start | bytes 1572868
  11.3 5.2 %copy-start.3 = (s32[4,8,128]{2,1,0:T(8,128)S(1)}, s32[4,8,128]{2,1,0:T(8,128)}, u32[]{:S(2)}) copy-start(s32[4,8,128]{2,1,0:T(8,128)} %pair_index.1.index_ref) | copy-start | bytes 49156
  12.2 11.6 %collective-permute-start.2 = (bf16[42,16,128]{2,1,0:T(8,128)(2,1)S(1)}, bf16[42,16,128]{2,1,0:T(8,128)(2,1)S(1)}, u32[]{:S(2)}, u32[]{:S(2)}) collective-permute-start(bf16[42,16,128]{2,1,0:T(8,128)(2,1)S(1)} %get-tuple-element.13), channel_id=1, source_target_pairs={{0,3},{1,2},{2,1},{3,0},{4,7},{5,6},{6,5},{7,4},{8,11},{9,10},{10,... | collective-permute-start | bytes 516104 | tf_op jit(solution)/shard_map/ppermute | solution.py:323
  16.5 7.3 %copy-start.2 = (bf16[8,128,128]{2,1,0:T(8,128)(2,1)S(1)}, bf16[8,128,128]{2,1,0:T(8,128)(2,1)}, u32[]{:S(2)}) copy-start(bf16[8,128,128]{2,1,0:T(8,128)(2,1)} %refs_5_.1) | copy-start | bytes 786436
  16.5 7.3 %collective-permute-start.4 = (bf16[42,16,128]{2,1,0:T(8,128)(2,1)S(1)}, bf16[42,16,128]{2,1,0:T(8,128)(2,1)S(1)}, u32[]{:S(2)}, u32[]{:S(2)}) collective-permute-start(bf16[42,16,128]{2,1,0:T(8,128)(2,1)S(1)} %get-tuple-element.15), channel_id=1, source_target_pairs={{0,1},{1,0},{2,3},{3,2},{4,5},{5,4},{6,7},{7,6},{8,9},{9,8},{10,11... | collective-permute-start | bytes 516104 | tf_op jit(solution)/shard_map/ppermute | solution.py:323
